TPU v7x, 32 devices: a whole 2x2x4 slice. The times are simulated.
32 devices in a mesh: fsdp: 8 (over z, x), rep: 2 (over y), ctx: 2 (over core).
Axes of the slice: x: 2, y: 2, z: 4, core: 2. Of those that a mesh axis runs over, the one named last changes fastest.
Arguments:
- tokens: bfloat16 [16, 1024, 1088], P(('fsdp', 'rep'), 'ctx'), may hold values from -6 to 6
- prefix_len: int32 [16], P(('fsdp', 'rep')), may hold values from 102 to 512
- ln1_gain: bfloat16 [1088], P('fsdp'), may hold values from 0.099609375 to 1.8984375
- ln1_bias: bfloat16 [1088], P('fsdp'), may hold values from -2 to 2
- w_qkv: bfloat16 [1088, 3264], P('fsdp'), may hold values from -0.1875 to 0.1875
- b_qv: bfloat16 [2176], P('fsdp'), may hold values from -2 to 2
- w_out: bfloat16 [1088, 1088], P('fsdp'), may hold values from -3 to 3
- b_out: bfloat16 [1088], P('fsdp'), may hold values from -2 to 2
- ln2_gain: bfloat16 [1088], P('fsdp'), may hold values from 0.099609375 to 1.8984375
- ln2_bias: bfloat16 [1088], P('fsdp'), may hold values from -2 to 2
- w_up: bfloat16 [1088, 4352], P('fsdp'), may hold values from -0.1875 to 0.1875
- b_up: bfloat16 [4352], P('fsdp'), may hold values from -2 to 2
- w_down: bfloat16 [4352, 1088], P('fsdp'), may hold values from -0.125 to 0.125
- b_down: bfloat16 [1088], P('fsdp'), may hold values from -2 to 2
- cotangent: bfloat16 [16, 1024, 1088], P(('fsdp', 'rep'), 'ctx'), may hold values from -6 to 6
Outputs:
- block_out: bfloat16 [16, 1024, 1088], P(('fsdp', 'rep'), 'ctx')
- grad_tokens: float32 [16, 1024, 1088], P(('fsdp', 'rep'), 'ctx')
- grad_ln1_gain: float32 [1088], P('fsdp')
- grad_ln1_bias: float32 [1088], P('fsdp')
- grad_w_qkv: float32 [1088, 3264], P('fsdp')
- grad_b_qv: float32 [2176], P('fsdp')
- grad_w_out: float32 [1088, 1088], P('fsdp')
- grad_b_out: float32 [1088], P('fsdp')
- grad_ln2_gain: float32 [1088], P('fsdp')
- grad_ln2_bias: float32 [1088], P('fsdp')
- grad_w_up: float32 [1088, 4352], P('fsdp')
- grad_b_up: float32 [4352], P('fsdp')
- grad_w_down: float32 [4352, 1088], P('fsdp')
- grad_b_down: float32 [1088], P('fsdp')
All inputs are finite; a program needn't handle non-finite values.
Results may differ from a plain program's by a relative error of at most 0.013.
Values may be sent and summed in bfloat16 or wider, within the bound.
No kernel may reach another device: no remote copies, remote signals or barrier semaphores. Data moves between devices by JAX's collectives and lax.ppermute only.
A program may use at most 192 MiB of HBM per device.

v0:
```python
import jax
import jax.numpy as jnp
from jax import lax
from jax.experimental import pallas as pl
from jax.experimental.pallas import tpu as pltpu
from jax.sharding import PartitionSpec as P

HD=64
QB=256
LOG2E=1.4426950408889634
NEG=-1e30

def dot_nn(a,b): return lax.dot_general(a,b,(((1,),(0,)),((),())),preferred_element_type=jnp.float32)
def dot_nt(a,b): return lax.dot_general(a,b,(((1,),(1,)),((),())),preferred_element_type=jnp.float32)
def dot_tn(a,b): return lax.dot_general(a,b,(((0,),(0,)),((),())),preferred_element_type=jnp.float32)

def key_extent(total, block):
    return max(total // 2, (block + 1) * QB)

def scores_t(keys, query, block, prefix, scale):
    raw = dot_nn(keys, query) * scale
    extent = raw.shape[0]
    free = block * QB
    if free:
        top, low = raw[:free], raw[free:]
    else:
        top, low = None, raw
    kpos = free + lax.broadcasted_iota(jnp.int32, low.shape, 0)
    qpos = free + lax.broadcasted_iota(jnp.int32, low.shape, 1)
    limit = jnp.maximum(qpos, prefix - 1)
    low = jnp.where(kpos <= limit, low, NEG)
    return low if top is None else jnp.concatenate([top, low], axis=0)

def fwd_kernel(info, q_ref, k_ref, v_ref, o_ref, l_ref):
    prefix = info[2]
    total = q_ref.shape[-1]
    keys = jnp.transpose(k_ref[0].astype(jnp.float32)).astype(jnp.bfloat16)
    scale = HD ** -0.5 * LOG2E
    for b in range(total // QB):
        ext = key_extent(total, b)
        sl = slice(b * QB, (b + 1) * QB)
        s = scores_t(keys[:ext], q_ref[0, :, sl], b, prefix, scale)
        top = jnp.max(s, axis=0, keepdims=True)
        p = jnp.exp2(s - top)
        denom = jnp.sum(p, axis=0, keepdims=True)
        mixed = dot_nn(v_ref[0, :, :ext], p.astype(jnp.bfloat16))
        o_ref[0, :, sl] = (mixed / denom).astype(jnp.bfloat16)
        l_ref[0, :, sl] = top + jnp.log2(denom)

def bwd_kernel(info, q_ref, k_ref, v_ref, o_ref, g_ref, l_ref, out_ref, dk_acc, dv_acc):
    prefix = info[2]
    total = q_ref.shape[-1]
    factor = HD ** -0.5
    scale = factor * LOG2E
    keep = jnp.where((info[3] == 0) & (pl.program_id(0) == pl.num_programs(0) - 1), 0.0, 1.0).astype(jnp.float32)
    keys_t = k_ref[0]
    keys = jnp.transpose(keys_t.astype(jnp.float32)).astype(jnp.bfloat16)
    values = jnp.transpose(v_ref[0].astype(jnp.float32)).astype(jnp.bfloat16)
    dk_acc[...] = jnp.zeros_like(dk_acc)
    dv_acc[...] = jnp.zeros_like(dv_acc)
    for b in range(total // QB):
        ext = key_extent(total, b)
        sl = slice(b * QB, (b + 1) * QB)
        query = q_ref[0, :, sl]
        grad = g_ref[0, :, sl]
        delta = jnp.sum(grad.astype(jnp.float32) * o_ref[0, :, sl].astype(jnp.float32), axis=0, keepdims=True)
        s = scores_t(keys[:ext], query, b, prefix, scale)
        p = jnp.exp2(s - l_ref[0, :, sl])
        dp = dot_nn(values[:ext], grad)
        ds = (p * (dp - delta)).astype(jnp.bfloat16)
        dv_acc[:, :ext] += dot_nt(grad, p.astype(jnp.bfloat16))
        dk_acc[:, :ext] += dot_nt(query, ds)
        out_ref[info[0], 0, :, sl] = (dot_nn(keys_t[:, :ext], ds) * (factor * keep)).astype(jnp.bfloat16)
    out_ref[1, 0] = (dk_acc[...] * (factor * keep)).astype(jnp.bfloat16)
    out_ref[info[1], 0] = (dv_acc[...] * keep).astype(jnp.bfloat16)

def attend(proj, info, heads):
    total = proj.shape[-1]
    cube = proj.reshape(3 * heads, HD, total)
    blk = lambda f: pl.BlockSpec((1, HD, total), f)
    cost = pl.CostEstimate(flops=4*heads*total*total*HD, bytes_accessed=8*heads*HD*total, transcendentals=heads*total*total)
    return pl.pallas_call(
        fwd_kernel,
        out_shape=(jax.ShapeDtypeStruct((heads, HD, total), jnp.bfloat16), jax.ShapeDtypeStruct((heads, 1, total), jnp.float32)),
        grid_spec=pltpu.PrefetchScalarGridSpec(num_scalar_prefetch=1, grid=(heads,),
            in_specs=[blk(lambda h, i: (i[0]*heads+h,0,0)), blk(lambda h, i: (heads+h,0,0)), blk(lambda h, i: (i[1]*heads+h,0,0))],
            out_specs=[blk(lambda h, i: (h,0,0)), pl.BlockSpec((1,1,total), lambda h,i:(h,0,0))]),
        cost_estimate=cost, name="attend")(info, cube, cube, cube)

def attend_back(proj, info, mixed, grad, logs, heads):
    total = proj.shape[-1]
    cube = proj.reshape(3 * heads, HD, total)
    blk = lambda f: pl.BlockSpec((1, HD, total), f)
    own = lambda h, i: (h,0,0)
    cost = pl.CostEstimate(flops=10*heads*total*total*HD, bytes_accessed=16*heads*HD*total, transcendentals=heads*total*total)
    return pl.pallas_call(
        bwd_kernel,
        out_shape=jax.ShapeDtypeStruct((3, heads, HD, total), jnp.bfloat16),
        grid_spec=pltpu.PrefetchScalarGridSpec(num_scalar_prefetch=1, grid=(heads,),
            in_specs=[blk(lambda h, i: (i[0]*heads+h,0,0)), blk(lambda h, i: (heads+h,0,0)), blk(lambda h, i: (i[1]*heads+h,0,0)), blk(own), blk(own), pl.BlockSpec((1,1,total), own)],
            out_specs=pl.BlockSpec((3,1,HD,total), lambda h,i:(0,h,0,0)),
            scratch_shapes=[pltpu.VMEM((HD,total),jnp.float32)]*2),
        cost_estimate=cost, name="attend_back")(info, cube, cube, cube, mixed, grad, logs)


EPS = 1e-05
BF = jnp.bfloat16
F32 = jnp.float32


def product(left, right, left_dim, right_dim):
    return lax.dot_general(
        left, right, (((left_dim,), (right_dim,)), ((), ())), preferred_element_type=F32
    )


def moments(values):
    center = values - jnp.mean(values, axis=-1, keepdims=True)
    variance = jnp.mean(center * center, axis=-1, keepdims=True)
    inverse = lax.rsqrt(variance + EPS)
    return center * inverse, inverse


def norm_backward(grad, scaled, inverse, gain):
    inner = grad * gain
    return inverse * (
        inner
        - jnp.mean(inner, axis=-1, keepdims=True)
        - scaled * jnp.mean(inner * scaled, axis=-1, keepdims=True)
    )


def hold(values, *after):
    return lax.optimization_barrier((values, after))[0]


def assemble(info, arrays, jobs, shape):
    total, rows = len(arrays), shape[1]

    def kernel(info_ref, *refs):
        out, sems = refs[total], refs[total + 1]

        def span(column, size):
            if isinstance(column, tuple):
                return pl.ds(pl.multiple_of(info_ref[column[0]], 128), size)
            return slice(column, column + size)

        copies = [
            pltpu.make_async_copy(
                refs[place].at[(*lead, slice(0, rows), span(source, size))],
                out.at[info_ref[block], :, span(target, size)],
                sems.at[i],
            )
            for i, (place, lead, block, source, target, size) in enumerate(jobs)
        ]
        for copy in copies:
            copy.start()
        for copy in copies:
            copy.wait()

    anywhere = pl.BlockSpec(memory_space=pl.ANY)
    return pl.pallas_call(
        kernel,
        out_shape=jax.ShapeDtypeStruct(shape, arrays[0].dtype),
        grid_spec=pltpu.PrefetchScalarGridSpec(
            num_scalar_prefetch=1,
            grid=(1,),
            in_specs=[anywhere] * total,
            out_specs=pl.BlockSpec(shape, lambda i, s: (0, 0, 0)),
            scratch_shapes=[pltpu.SemaphoreType.DMA((len(jobs),))],
        ),
        cost_estimate=pl.CostEstimate(
            flops=0, bytes_accessed=4 * shape[0] * shape[1] * shape[2], transcendentals=0
        ),
        name="assemble",
    )(info, *arrays)


class Grid:
    def __init__(self):
        self.count = lax.axis_size("fsdp")
        self.near = 1 << ((self.count.bit_length() - 1) // 2)
        self.far = self.count // self.near
        self.reps = lax.axis_size("rep")
        self.split = self.reps == 2 and self.near == 2
        place = lax.axis_index("fsdp")
        self.zi = place // self.near
        self.xi = place % self.near
        self.y = lax.axis_index("rep")
        self.c = lax.axis_index("ctx")
        order = [k for pair in zip(range(1, self.far), range(self.far - 1, 0, -1)) for k in pair]
        self.steps = list(dict.fromkeys(order))

    def far_shift(self, array, k):
        near, far = self.near, self.far
        pairs = [(i, (i // near + k) % far * near + i % near) for i in range(self.count)]
        return lax.ppermute(array, "fsdp", pairs)

    def near_shift(self, array, k):
        near = self.near
        pairs = [(i, i // near * near + (i % near + k) % near) for i in range(self.count)]
        return lax.ppermute(array, "fsdp", pairs)

    def swap_rep(self, array):
        return lax.ppermute(array, "rep", [(0, 1), (1, 0)])

    def swap_ctx(self, array):
        return lax.ppermute(array, "ctx", [(0, 1), (1, 0)])

    def lines(self, piece):
        return [piece] + [self.far_shift(piece, k) for k in range(1, self.far)]

    def spots(self):
        return [
            (self.zi - k) % self.far * self.near + (self.xi - j) % self.near
            for j in range(self.near)
            for k in range(self.far)
        ]

    def gather_all(self, piece):
        return lax.all_gather(piece, "fsdp", axis=0, tiled=True)

    def scatter_all(self, grads):
        return lax.psum_scatter(grads, "fsdp", scatter_dimension=0, tiled=True)

    def groups(self):
        steps = sorted(range(1, self.far), key=lambda k: (abs(2 * k - self.far), k)) + [0]
        return steps[: self.far // 2], steps[self.far // 2 :]

    def pick_lines(self, cube, steps):
        return jnp.stack(
            [
                lax.dynamic_index_in_dim(cube, (self.zi + k) % self.far, 0, keepdims=False)
                for k in steps
            ]
        )

    def near_send(self, cube):
        return self.near_shift(
            lax.dynamic_index_in_dim(cube, (self.xi + 1) % self.near, 1, keepdims=False), 1
        )

    def line_sum(self, cube, arrived, at):
        tail = cube.shape[2:]
        own = lax.dynamic_slice(cube, (at, self.xi, 0, 0), (1, 1, *tail)).reshape(tail)
        other = lax.dynamic_index_in_dim(arrived, at, 0, keepdims=False)
        return own.astype(F32) + other.astype(F32)

    def near_sum(self, cube, arrived, k):
        return self.line_sum(cube, arrived, (self.zi + k) % self.far)

    def scatter(self, grads):
        cube = grads.reshape(self.far, self.near, *grads.shape[1:])
        arrived = self.near_send(cube)
        passed = [
            self.far_shift(self.near_sum(cube, arrived, k).astype(grads.dtype), k)
            for k in range(1, self.far)
        ]
        total = self.near_sum(cube, arrived, 0)
        for extra in passed:
            total += extra.astype(F32)
        return total

    def sum_rep(self, total):
        if self.split:
            return total.astype(F32) + self.swap_rep(total.astype(BF)).astype(F32)
        return lax.psum(total.astype(F32), "rep")


def shards(
    tokens,
    prefix_len,
    ln1_gain,
    ln1_bias,
    w_qkv,
    b_qv,
    w_out,
    b_out,
    ln2_gain,
    ln2_bias,
    w_up,
    b_up,
    w_down,
    b_down,
    cotangent,
):
    grid = Grid()
    count, c, y = grid.count, grid.c, grid.y
    first = c == 0
    seqs, rows, width = tokens.shape
    total_len = 2 * rows
    heads_all = width // HD
    heads = (heads_all + 1) // 2
    wide = heads * HD
    skip = width - wide
    part = width // count
    ff = w_up.shape[1]
    half_ff = ff // 2
    slab = ff // count // 2
    own_tokens = tokens.reshape(rows, width)
    own_cot = cotangent.reshape(rows, width)
    lead = (y == 0) if grid.split else True

    def choose(flag, a, b):
        return a if flag is True else jnp.where(flag, a, b)

    def both(own, other):
        return jnp.where(
            first,
            jnp.concatenate([own, other], axis=0),
            jnp.concatenate([other, own], axis=0),
        )

    small = [ln1_gain, ln1_bias, b_qv, b_out, ln2_gain, ln2_bias, b_up, b_down]
    sizes = [v.shape[0] for v in small]
    vec = jnp.concatenate(small)

    def section(k):
        low = w_qkv[:, k * width : k * width + wide]
        return jnp.where(first, low, w_qkv[:, k * width + skip : k * width + skip + wide])

    w_q, w_k, w_v = section(0), section(1), section(2)
    down_own = lax.dynamic_slice(w_down, (slab * c, 0), (slab, width))
    out_own = lax.dynamic_slice(w_out, (0, skip * c), (part, wide))
    up_cols = w_up.reshape(part, count, 2, slab)
    up_own = lax.dynamic_index_in_dim(up_cols, c, 2, keepdims=False).reshape(part, half_ff)
    up_skip = half_ff // 2 // 128 * 128
    up_wide = half_ff - up_skip
    if grid.split:
        far = grid.far
        mine = jnp.where(lead, w_q, w_v)
        tail_rows = -(-vec.shape[0] // (2 * wide))
        tail = jnp.pad(vec, (0, 8 * 2 * wide - vec.shape[0])).reshape(8, 2 * wide)
        lines = grid.lines(
            jnp.concatenate([jnp.concatenate([mine, w_k], axis=1), tail], axis=0)
        )
        up_cut = lambda rep: lax.dynamic_slice(up_own, (0, up_skip * rep), (part, up_wide))
        lines, up_mine, out_own, down_own = hold((lines, up_cut(y), out_own, down_own))
        half_out = grid.gather_all(out_own)
        full_down = grid.gather_all(down_own)
        qkv_near = jnp.stack(lines)
        qkv_next = grid.near_shift(qkv_near, 1)
        up_lines = grid.lines(up_mine)
        qkv_near, qkv_next, up_lines = hold((qkv_near, qkv_next, up_lines))
        qkv_other = grid.swap_rep(
            jnp.stack([qkv_near[:, :part, :wide], qkv_next[:, :part, :wide]])
        )
        up_near = jnp.stack(up_lines)
        up_next = grid.near_shift(up_near, 1)
        qkv_near, qkv_next, qkv_other, up_near, up_next = hold(
            (qkv_near, qkv_next, qkv_other, up_near, up_next)
        )
        spots = jnp.stack(
            grid.spots() + [up_skip * y, (up_wide - up_skip) * (1 - y), up_wide * (1 - y)]
        ).astype(jnp.int32)
        full_qkv = assemble(
            spots,
            [qkv_near, qkv_next, qkv_other],
            [(i // far, (i % far,), i, 0, 0, 2 * wide) for i in range(count)]
            + [(2, (i // far, i % far), i, 0, 2 * wide, wide) for i in range(count)],
            (count, part, 3 * wide),
        )
        tails = jnp.concatenate([qkv_near, qkv_next])[:, part : part + tail_rows]
        chosen = spots[None, :count, None] == jnp.arange(count)[:, None, None]
        vec_full = jnp.sum(
            jnp.where(chosen, tails.reshape(1, count, -1).astype(F32), 0.0), axis=1
        )
        up_other = grid.swap_rep(jnp.stack([up_near, up_next]))
    else:
        full_qkv = grid.gather_all(jnp.concatenate([w_q, w_k, w_v], axis=1))
        vec_full = grid.gather_all(vec.reshape(1, -1)).astype(F32)
        half_out = grid.gather_all(out_own)
        full_up = grid.gather_all(up_own)
        full_down = grid.gather_all(down_own)
    full_qkv = full_qkv.reshape(width, 3 * wide)
    small_full, at = [], 0
    for size in sizes:
        small_full.append(vec_full[:, at : at + size].reshape(-1))
        at += size
    gain_one, shift_one, bias_qv, bias_out, gain_two, shift_two, bias_up, bias_down = small_full

    all_tokens = both(own_tokens, grid.swap_ctx(own_tokens))
    all_cot = both(own_cot, grid.swap_ctx(own_cot))
    inputs = all_tokens.astype(F32)
    scaled_one, _ = moments(inputs)
    normed = (scaled_one * gain_one + shift_one).astype(BF)
    bias_q = lax.dynamic_slice(bias_qv, (skip * c,), (wide,))
    bias_v = lax.dynamic_slice(bias_qv, (width + skip * c,), (wide,))
    bias_row = jnp.concatenate(
        [choose(lead, bias_q, bias_v), jnp.zeros((wide,), F32), choose(lead, bias_v, bias_q)]
    )
    project = (product(full_qkv, normed, 0, 1) + bias_row[:, None]).astype(BF)
    flip = jnp.int32(0) if lead is True else jnp.where(lead, 0, 2).astype(jnp.int32)
    info = jnp.stack([flip, 2 - flip, prefix_len[0], c.astype(jnp.int32)])
    mixed, logs = attend(project, info, heads)
    other_out = grid.swap_ctx(half_out)
    full_out = jnp.concatenate(
        [jnp.where(first, half_out, other_out)[:, :skip], jnp.where(first, other_out, half_out)],
        axis=1,
    )
    bias_up_own = lax.dynamic_index_in_dim(bias_up.reshape(count, 2, slab), c, 1, keepdims=False)
    bias_up_own = bias_up_own.reshape(half_ff)
    own_mixed = mixed.reshape(wide, total_len)
    other_mixed = grid.swap_ctx(own_mixed)
    overlap = wide - skip
    attended = jnp.where(
        first,
        jnp.concatenate([own_mixed, other_mixed[overlap:]], axis=0),
        jnp.concatenate([other_mixed, own_mixed[overlap:]], axis=0),
    )

    middle = inputs + product(attended, full_out, 0, 0) + bias_out
    if grid.split:
        middle, up_other = hold((middle, up_other))
        full_up = assemble(
            spots,
            [up_near, up_next, up_other],
            [(i // far, (i % far,), i, 0, (count,), up_wide) for i in range(count)]
            + [
                (2, (i // far, i % far), i, (count + 1,), (count + 2,), up_skip)
                for i in range(count)
            ],
            (count, part, half_ff),
        ).reshape(width, half_ff)
    scaled_two, inverse_two = moments(middle)
    hidden_in = (scaled_two * gain_two + shift_two).astype(BF)
    pre = product(hidden_in, full_up, 1, 0) + bias_up_own
    cdf = 0.5 + 0.5 * lax.erf(pre * (0.5**0.5))
    activated = (pre * cdf).astype(BF)
    slope = (cdf + pre * jnp.exp(-0.5 * pre * pre) * (0.5 / jnp.pi) ** 0.5).astype(BF)

    own_rows = lambda array: lax.dynamic_slice(array, (rows * c, 0), (rows, array.shape[1]))
    other_rows = lambda array: lax.dynamic_slice(
        array, (rows * (1 - c), 0), (rows, array.shape[1])
    )

    grad_down = product(activated, all_cot, 0, 0).astype(BF)
    full_down, grad_down = hold((full_down, grad_down))
    grad_act = product(all_cot, full_down, 1, 1)
    grad_pre = (grad_act * slope.astype(F32)).astype(BF)
    if grid.split:
        own_down = grid.scatter_all(grad_down)
        grad_cut = lambda rep: lax.dynamic_slice(grad_pre, (0, up_skip * rep), (total_len, up_wide))
        up_sent = product(hidden_in, grad_cut(1 - y), 0, 0).astype(BF)
        up_mine = product(hidden_in, grad_cut(y), 0, 0).astype(BF)
        rows_cube = lambda g: g.reshape(far, grid.near, part, g.shape[1])
        groups = grid.groups()
        up_sent, up_mine = rows_cube(up_sent), rows_cube(up_mine)
        up_sent = [grid.swap_rep(grid.pick_lines(up_sent, steps)) for steps in groups]
    else:
        own_down = grid.scatter_all(grad_down)
        grad_up = product(hidden_in, grad_pre, 0, 0).astype(BF)
    grad_hidden = product(grad_pre, full_up, 1, 1)
    if grid.split:
        grad_hidden, up_mine, up_sent[0], activated = hold(
            (grad_hidden, up_mine, up_sent[0], activated)
        )
        merge = lambda i: (
            grid.pick_lines(up_mine, groups[i]).astype(F32) + up_sent[i].astype(F32)
        ).astype(BF)
        up_cubes = [merge(0)]
        up_near = [grid.near_send(up_cubes[0])]
    partial_down = product(activated, full_down, 1, 0)
    result = own_rows(partial_down) + grid.swap_ctx(other_rows(partial_down))
    block_out = (own_rows(middle) + result + bias_down).astype(BF).reshape(seqs, rows, width)
    grad_hidden = grad_hidden + grid.swap_ctx(grad_hidden)
    grad_middle = all_cot.astype(F32) + norm_backward(grad_hidden, scaled_two, inverse_two, gain_two)
    grad_branch = grad_middle.astype(BF)
    if grid.split:
        grad_branch, up_near, up_cubes, block_out = hold(
            (grad_branch, up_near, up_cubes, block_out)
        )
        send_far = lambda i: {
            k: grid.far_shift(grid.line_sum(up_cubes[i], up_near[i], at).astype(BF), k)
            for at, k in enumerate(groups[i])
            if k
        }
        up_far = send_far(0)
    branch_cols = lax.dynamic_slice(grad_branch, (0, skip * c), (total_len, wide))
    grad_wout = product(attended, branch_cols, 1, 0).astype(BF)
    out_rows = lax.dynamic_slice(full_out, (skip * c, 0), (wide, width))
    grad_mixed = product(out_rows, grad_branch, 1, 1).astype(BF).reshape(heads, HD, total_len)
    if grid.split:
        up_sent[1], grad_wout, grad_mixed = hold((up_sent[1], grad_wout, grad_mixed))
        up_cubes.append(merge(1))
        up_near.append(grid.near_send(up_cubes[1]))
        out_cube = rows_cube(grad_wout)
        out_near = grid.near_send(out_cube)
    grad_cube = attend_back(project, info, mixed, grad_mixed, logs, heads)
    if grid.split:
        grad_cube, up_near, up_cubes, up_far, out_near, out_cube = hold(
            (grad_cube, up_near, up_cubes, up_far, out_near, out_cube)
        )
        up_far.update(send_far(1))
        out_far = [
            grid.far_shift(grid.near_sum(out_cube, out_near, k).astype(BF), k)
            for k in range(1, far)
        ]
    grad_project = grad_cube.reshape(3 * wide, total_len)
    qkv_sent = product(normed, grad_project[2 * wide :], 0, 1).astype(BF)
    qkv_mine = product(normed, grad_project[: 2 * wide], 0, 1).astype(BF)
    if grid.split:
        qkv_sent, qkv_mine, grad_project = hold((qkv_sent, qkv_mine, grad_project))
        qkv_sent = grid.swap_rep(qkv_sent)
        key_cube = rows_cube(qkv_mine[:, wide:])
        key_near = grid.near_send(key_cube)
    grad_normed = product(grad_project, full_qkv, 0, 1)
    own_grad = own_rows(grad_normed) + grid.swap_ctx(other_rows(grad_normed))
    own_scaled, own_inverse = moments(own_tokens.astype(F32))
    grad_tokens = own_rows(grad_middle) + norm_backward(own_grad, own_scaled, own_inverse, gain_one)
    grad_tokens = grad_tokens.reshape(seqs, rows, width)

    if grid.split:
        qkv_sent, qkv_mine, key_near, key_cube, up_far, out_far, own_grad = hold(
            (qkv_sent, qkv_mine, key_near, key_cube, up_far, out_far, own_grad)
        )
        low = qkv_mine[:, :wide].astype(F32) + qkv_sent.astype(F32)
        low_cube = rows_cube(low.astype(BF))
        low_near = grid.near_send(low_cube)
        key_far = [
            grid.far_shift(grid.near_sum(key_cube, key_near, k).astype(BF), k)
            for k in range(1, far)
        ]
        up_total = grid.line_sum(up_cubes[1], up_near[1], far - far // 2 - 1)
        for extra in up_far.values():
            up_total += extra.astype(F32)
        out_total = grid.near_sum(out_cube, out_near, 0)
        for extra in out_far:
            out_total += extra.astype(F32)
        pair = jnp.concatenate([up_total.astype(BF), out_total.astype(BF)], axis=1)
        pair_other = grid.swap_rep(pair)
        low_near, low_cube, pair, pair_other, key_far = hold(
            (low_near, low_cube, pair, pair_other, key_far)
        )
        low_far = [
            grid.far_shift(grid.near_sum(low_cube, low_near, k).astype(BF), k)
            for k in range(1, far)
        ]
    own_down = grid.sum_rep(own_down).astype(BF)
    other_down = grid.swap_ctx(own_down)
    out_down = jnp.where(
        first,
        jnp.concatenate([own_down, other_down], axis=0),
        jnp.concatenate([other_down, own_down], axis=0),
    ).astype(F32)

    if grid.split:
        mine, other = pair[:, :up_wide], pair_other[:, :up_wide]
        own_up = jnp.concatenate(
            [jnp.where(lead, mine, other)[:, :up_skip], jnp.where(lead, other, mine)], axis=1
        )
    else:
        own_up = grid.sum_rep(grid.scatter_all(grad_up)).astype(BF)
    other_up = grid.swap_ctx(own_up)
    weave = lambda a, b: jnp.stack(
        [a.reshape(part, count, slab), b.reshape(part, count, slab)], axis=2
    ).reshape(part, ff)
    out_up = weave(
        jnp.where(first, own_up, other_up), jnp.where(first, other_up, own_up)
    ).astype(F32)

    if grid.split:
        own_wout = (pair[:, up_wide:].astype(F32) + pair_other[:, up_wide:].astype(F32)).astype(BF)
    else:
        own_wout = grid.sum_rep(grid.scatter_all(grad_wout)).astype(BF)
    other_wout = grid.swap_ctx(own_wout)
    out_wout = jnp.concatenate(
        [jnp.where(first, own_wout, other_wout)[:, :skip], jnp.where(first, other_wout, own_wout)],
        axis=1,
    ).astype(F32)

    if grid.split:
        keys = grid.near_sum(key_cube, key_near, 0)
        for extra in key_far:
            keys += extra.astype(F32)
        centre = grid.sum_rep(keys).astype(BF)
        low_far, out_up, out_wout, out_down, centre = hold(
            (low_far, out_up, out_wout, out_down, centre)
        )
        mine = grid.near_sum(low_cube, low_near, 0)
        for extra in low_far:
            mine += extra.astype(F32)
        mine = mine.astype(BF)
        other = grid.swap_rep(mine)
        own_sections = [
            jnp.where(lead, mine, other),
            centre,
            jnp.where(lead, other, mine),
        ]
    else:
        own_qkv = [grid.sum_rep(grid.scatter_all(g)).astype(BF) for g in (qkv_mine, qkv_sent)]
        own_sections = [own_qkv[0][:, :wide], own_qkv[0][:, wide:], own_qkv[1]]
    own_qkv = jnp.concatenate(own_sections, axis=1)
    other_qkv = grid.swap_ctx(own_qkv)
    low_qkv = jnp.where(first, own_qkv, other_qkv)
    high_qkv = jnp.where(first, other_qkv, own_qkv)
    pieces = []
    for k in range(3):
        pieces.append(low_qkv[:, k * wide : k * wide + skip])
        pieces.append(high_qkv[:, k * wide : (k + 1) * wide])
    out_qkv = jnp.concatenate(pieces, axis=1).astype(F32)

    once = jnp.where(first, 1.0, 0.0).astype(F32)
    spread = lambda values, start, size: lax.dynamic_update_slice(
        jnp.zeros((size,), F32), values, (start,)
    )
    project_sums = jnp.sum(grad_cube.astype(F32), axis=3).reshape(3, wide)
    sums_q = choose(lead, project_sums[0], project_sums[2])
    sums_v = choose(lead, project_sums[2], project_sums[0])
    grad_bias_qv = jnp.concatenate(
        [spread(sums_q, skip * c, width), spread(sums_v, skip * c, width)]
    )
    pre_sums = jnp.sum(grad_pre.astype(F32), axis=0).reshape(count, slab)
    grad_bias_up = lax.dynamic_update_slice(
        jnp.zeros((count, 2, slab), F32), pre_sums[:, None], (0, c, 0)
    )
    vectors = [
        jnp.sum(own_grad * own_scaled, axis=0),
        jnp.sum(own_grad, axis=0),
        grad_bias_qv,
        once * jnp.sum(grad_branch.astype(F32), axis=0),
        once * jnp.sum(grad_hidden * scaled_two, axis=0),
        once * jnp.sum(grad_hidden, axis=0),
        grad_bias_up,
        once * jnp.sum(all_cot.astype(F32), axis=0),
    ]
    table = jnp.concatenate([v.reshape(count, -1) for v in vectors], axis=1)
    table = table + grid.swap_ctx(table)
    table = table + grid.swap_rep(table) if grid.split else lax.psum(table, "rep")
    summed = grid.scatter(table[:, None, :]).reshape(-1)
    outs, at = [], 0
    for size in sizes:
        outs.append(summed[at : at + size])
        at += size
    return (
        block_out,
        grad_tokens,
        outs[0],
        outs[1],
        out_qkv,
        outs[2],
        out_wout,
        outs[3],
        outs[4],
        outs[5],
        out_up,
        outs[6],
        out_down,
        outs[7],
    )


def solution(mesh):
    placed = (
        P(("fsdp", "rep"), "ctx", None),
        P(("fsdp", "rep")),
        P("fsdp"),
        P("fsdp"),
        P("fsdp", None),
        P("fsdp"),
        P("fsdp", None),
        P("fsdp"),
        P("fsdp"),
        P("fsdp"),
        P("fsdp", None),
        P("fsdp"),
        P("fsdp", None),
        P("fsdp"),
        P(("fsdp", "rep"), "ctx", None),
    )
    return jax.shard_map(
        shards,
        mesh=mesh,
        in_specs=placed,
        out_specs=(
            P(("fsdp", "rep"), "ctx", None),
            P(("fsdp", "rep"), "ctx", None),
            P("fsdp"),
            P("fsdp"),
            P("fsdp", None),
            P("fsdp"),
            P("fsdp", None),
            P("fsdp"),
            P("fsdp"),
            P("fsdp"),
            P("fsdp", None),
            P("fsdp"),
            P("fsdp", None),
            P("fsdp"),
        ),
        check_vma=False,
    )
```

profile of v0, /device:TPU:0, one launch (start us, length us, event | category | flops | bytes accessed | tf_op | source)
XLA Modules:
  0.0 555.0 jit_solution(3496770463434726637)
XLA Ops:
  21.6 6.4 %reshape.407 = bf16[136,8,2,272]{3,2,1,0:T(2,128)(2,1)} reshape(bf16[136,4352]{1,0:T(8,128)(2,1)} %param.25) | data formatting | bytes 2367488 | tf_op jit(solution)/shard_map/reshape | solution.py:325
  27.9 6.7 %dynamic-slice_reduce_fusion = bf16[136,8,272]{2,1,0:T(8,128)(2,1)S(1)} fusion(bf16[136,8,2,272]{3,2,1,0:T(2,128)(2,1)} %reshape.407, s32[]{:T(128)S(6)} %select_n.425), kind=kLoop, calls=%fused_computation.68 | loop fusion | bytes 1183748 | tf_op jit(solution)/shard_map/jit(dynamic_index_in_dim)/dynamic_slice | solution.py:326
  45.9 7.6 %collective-permute-start.6 = (bf16[136,1152]{1,0:T(8,128)(2,1)}, bf16[136,1152]{1,0:T(8,128)(2,1)S(1)}, u32[]{:S(2)}, u32[]{:S(2)}) collective-permute-start(bf16[136,1152]{1,0:T(8,128)(2,1)} %constant_dynamic-slice_fusion.21), channel_id=1, source_target_pairs={{0,8},{4,12},{8,16},{12,20},{16,24},{20,28},{24,0},{28,4},{1,9},{5... | collective-permute-start | bytes 940040 | tf_op jit(solution)/shard_map/ppermute | solution.py:197
  56.1 7.2 %collective-permute-done.6 = bf16[136,1152]{1,0:T(8,128)(2,1)S(1)} collective-permute-done((bf16[136,1152]{1,0:T(8,128)(2,1)}, bf16[136,1152]{1,0:T(8,128)(2,1)S(1)}, u32[]{:S(2)}, u32[]{:S(2)}) %collective-permute-start.6) | collective-permute-done | bytes 313376 | tf_op jit(solution)/shard_map/ppermute | solution.py:197
  63.3 16.8 %collective-permute-done.7 = bf16[136,1152]{1,0:T(8,128)(2,1)S(1)} collective-permute-done((bf16[136,1152]{1,0:T(8,128)(2,1)}, bf16[136,1152]{1,0:T(8,128)(2,1)S(1)}, u32[]{:S(2)}, u32[]{:S(2)}) %collective-permute-start.7) | collective-permute-done | bytes 313376 | tf_op jit(solution)/shard_map/ppermute | solution.py:197
  90.9 24.9 %all-gather.3.cloned.1.call-done = bf16[1088,576]{1,0:T(8,128)(2,1)} async-done(((bf16[136,576]{1,0:T(8,128)(2,1)}), bf16[1088,576]{1,0:T(8,128)(2,1)}) %all-gather.3.cloned.1.call-update) | async-done | bytes 1253392 | tf_op jit(solution)/shard_map/all_gather | solution.py:221
  130.6 9.1 %add_convert_fusion = bf16[1728,1024]{1,0:T(8,128)(2,1)} fusion(bf16[1088,1728]{1,0:T(8,128)(2,1)} %bitcast.262, f32[1728]{0:T(1024)S(1)} %concatenate.77, f32[1088]{0:T(1024)S(1)} %add.560, f32[1088]{0:T(1024)S(1)} %mul.224, f32[1024]{0:T(1024)S(1)} %add_rsqrt_fusion.1, f32[1024]{0:T(1024)S(1)} %broadcast_multiply_fusion.7, ...), kind=kOutput, calls=%fused_computation.15 | convolution fusion | flops 3870621696 | bytes 9551105 | tf_op jit(solution)/shard_map/dot_general | solution.py:112
  139.8 22.0 %attend.1 = (bf16[9,64,1024]{2,1,0:T(8,128)(2,1)}, f32[9,1,1024]{2,1,0:T(1,128)}) custom-call(s32[4]{0:T(128)} %pad_add_fusion.info, bf16[27,64,1024]{2,1,0:T(8,128)(2,1)} %bitcast.282, bf16[27,64,1024]{2,1,0:T(8,128)(2,1)} %bitcast.283, bf16[27,64,1024]{2,1,0:T(8,128)(2,1)} %bitcast.284), custom_call_target="tpu_custom_call" | custom-call | flops 2415919104 | bytes 4718592 | tf_op jit(solution)/shard_map/attend/pallas_call | solution.py:82
  172.6 6.9 %fusion.7 = f32[1024,1088]{0,1:T(8,128)} fusion(bf16[1088,512]{1,0:T(8,128)(2,1)S(1)} %slice_select_fusion, bf16[1088,576]{1,0:T(8,128)(2,1)S(1)} %broadcast_select_fusion, f32[1088]{0:T(1024)S(1)} %add.568, bf16[512,1024]{1,0:T(8,128)(2,1)S(1)} %slice.241, bf16[576,1024]{1,0:T(8,128)(2,1)S(1)} %bitcast.270, bf16[512,1024]{1,0:T(8,128)(2,1)S(1)} %bitcast.267, ...), kind=kOutput, calls=%fused_computation.23 | convolution fusion | flops 2452439040 | bytes 13512961 | tf_op jit(solution)/shard_map/dot_general | solution.py:112
  194.1 9.2 %multiply_convert_fusion.1 = (bf16[1024,2176]{1,0:T(8,128)(2,1)S(1)}, f32[1024,2176]{1,0:T(8,128)}) fusion(f32[2176]{0:T(1024)S(1)} %add.575, bf16[1024,1088]{0,1:T(8,128)(2,1)S(1)} %add_convert_fusion.1, bf16[1088,2176]{1,0:T(8,128)(2,1)S(1)} %bitcast.258), kind=kOutput, calls=%fused_computation.9 | convolution fusion | flops 4861984768 | bytes 20341248 | tf_op jit(solution)/shard_map/dot_general | solution.py:112
  205.6 10.0 %convolution_convert_fusion = bf16[2176,1088]{0,1:T(8,128)(2,1)} fusion(bf16[1024,2176]{1,0:T(8,128)(2,1)S(1)} %get-tuple-element.109, bf16[512,1088]{0,1:T(8,128)(2,1)} %collective-permute-done, bf16[512,1088]{0,1:T(8,128)(2,1)} %bitcast, pred[]{:T(512)S(6)} %eq.72), kind=kOutput, calls=%fused_computation.1 | convolution fusion | flops 4861009920 | bytes 11419649 | tf_op jit(solution)/shard_map/dot_general | solution.py:112
  215.6 13.1 %convert_reduce_fusion = (f32[2176]{0:T(1024)S(1)}, bf16[1024,2176]{1,0:T(8,128)(2,1)S(1)}) fusion(f32[1024,2176]{1,0:T(8,128)} %get-tuple-element.294, f32[2176]{0:T(1024)S(1)} %add.575, bf16[2176,1088]{1,0:T(8,128)(2,1)} %all-gather.5.cloned.1.call-done, bf16[512,1088]{0,1:T(8,128)(2,1)} %collective-permute-done, bf16[512,1088]{0,1:T(8,128)(2,1)} %bitcast, ...), kind=kOutput, calls=%fused_computation.7 | convolution fusion | flops 4892063744 | bytes 20349952 | tf_op jit(solution)/shard_map/dot_general | solution.py:112
  237.5 7.0 %fusion.92 = f32[1024,1088]{0,1:T(8,128)} fusion(bf16[1024,2176]{1,0:T(8,128)(2,1)S(1)} %get-tuple-element.296, bf16[1088,2176]{1,0:T(8,128)(2,1)S(1)} %bitcast.261), kind=kOutput, calls=%fused_computation.230 | convolution fusion | flops 4848615424 | bytes 13647872 | tf_op jit(solution)/shard_map/dot_general | solution.py:112
  244.4 18.0 %collective-permute-done.14 = bf16[2,2,136,1152]{3,2,1,0:T(8,128)(2,1)} collective-permute-done((bf16[2,2,136,1152]{3,2,1,0:T(8,128)(2,1)S(1)}, bf16[2,2,136,1152]{3,2,1,0:T(8,128)(2,1)}, u32[]{:S(2)}, u32[]{:S(2)}) %collective-permute-start.14) | collective-permute-done | bytes 1253408 | tf_op jit(solution)/shard_map/ppermute | solution.py:205
  262.4 9.3 %fusion.93 = f32[1024,1088]{0,1:T(8,128)S(1)} fusion(bf16[1024,2176]{1,0:T(8,128)(2,1)} %copy-done.59, bf16[2176,1088]{1,0:T(8,128)(2,1)} %all-gather.5.cloned.1.call-done), kind=kOutput, calls=%fused_computation.231 | convolution fusion | flops 4848615424 | bytes 13647872 | tf_op jit(solution)/shard_map/dot_general | solution.py:112
  278.2 8.3 %copy.87 = bf16[2176,1088]{1,0:T(8,128)(2,1)} copy(bf16[2176,1088]{0,1:T(8,128)(2,1)} %convolution_convert_fusion) | data formatting | bytes 9469952
  301.7 6.8 %fusion.86 = (bf16[1024,1088]{0,1:T(8,128)(2,1)S(1)}, f32[1024,1088]{0,1:T(8,128)}, f32[1088]{0:T(1024)S(1)}) fusion(f32[1024]{0:T(1024)S(1)} %broadcast_multiply_fusion.4, f32[1024,1088]{0,1:T(8,128)S(1)} %bitcast.236, f32[1024]{0:T(1024)S(1)} %broadcast_multiply_fusion.6, f32[1024]{0:T(1024)S(1)} %broadcast_multiply_fusion.5, ...), kind=kLoop, calls=%fused_computation.224 | loop fusion | flops 22281152 | bytes 17850880 | tf_op jit(solution)/shard_map/convert_element_type | solution.py:468
  308.6 5.8 %collective-permute-done.16 = bf16[2,136,1152]{2,1,0:T(8,128)(2,1)S(1)} collective-permute-done((bf16[2,136,1152]{2,1,0:T(8,128)(2,1)S(1)}, bf16[2,136,1152]{2,1,0:T(8,128)(2,1)S(1)}, u32[]{:S(2)}, u32[]{:S(2)}) %collective-permute-start.16) | collective-permute-done | bytes 626720 | tf_op jit(solution)/shard_map/ppermute | solution.py:202
  328.8 7.0 %collective-permute-start.20 = (bf16[136,1152]{1,0:T(8,128)(2,1)}, bf16[136,1152]{1,0:T(8,128)(2,1)}, u32[]{:S(2)}, u32[]{:S(2)}) collective-permute-start(bf16[136,1152]{1,0:T(8,128)(2,1)} %get-tuple-element.255), channel_id=1, source_target_pairs={{0,8},{4,12},{8,16},{12,20},{16,24},{20,28},{24,0},{28,4},{1,9},{5... | collective-permute-start | bytes 940040 | tf_op jit(solution)/shard_map/ppermute | solution.py:197
  341.6 22.7 %attend_back.1 = bf16[3,9,64,1024]{3,2,1,0:T(8,128)(2,1)} custom-call(s32[4]{0:T(128)} %pad_add_fusion.info, bf16[27,64,1024]{2,1,0:T(8,128)(2,1)} %bitcast.285, bf16[27,64,1024]{2,1,0:T(8,128)(2,1)} %bitcast.286, bf16[27,64,1024]{2,1,0:T(8,128)(2,1)} %bitcast.287, bf16[9,64,1024]{2,1,0:T(8,128)(2,1)} %get-tuple-element.98.o_ref, ...), custom_call_target="tpu_custom_call" | custom-call | flops 6039797760 | bytes 9437184 | tf_op jit(solution)/shard_map/attend_back/pallas_call | solution.py:96
  369.9 6.1 %convolution_convert_fusion.1 = bf16[1088,1152]{0,1:T(8,128)(2,1)} fusion(bf16[1152,1024]{1,0:T(8,128)(2,1)S(1)} %bitcast.245, f32[1088]{0:T(1024)S(1)} %add.560, f32[1088]{0:T(1024)S(1)} %mul.224, f32[1024]{0:T(1024)S(1)} %add_rsqrt_fusion.1, f32[1024]{0:T(1024)S(1)} %broadcast_multiply_fusion.7, bf16[512,1088]{0,1:T(8,128)(2,1)S(1)} %bitcast.242, ...), kind=kOutput, calls=%fused_computation.11 | convolution fusion | flops 2584879104 | bytes 7111169 | tf_op jit(solution)/shard_map/dot_general | solution.py:112
  392.2 6.7 %collective-permute-start.27 = (bf16[136,576]{1,0:T(8,128)(2,1)}, bf16[136,576]{1,0:T(8,128)(2,1)S(1)}, u32[]{:S(2)}, u32[]{:S(2)}) collective-permute-start(bf16[136,576]{1,0:T(8,128)(2,1)} %get-tuple-element.253), channel_id=1, source_target_pairs={{0,8},{4,12},{8,16},{12,20},{16,24},{20,28},{24,0},{28,4},{1,9},{5... | collective-permute-start | bytes 470024 | tf_op jit(solution)/shard_map/ppermute | solution.py:197
  467.9 6.0 %collective-permute-done.39 = bf16[136,576]{1,0:T(8,128)(2,1)S(1)} collective-permute-done((bf16[136,576]{1,0:T(8,128)(2,1)S(1)}, bf16[136,576]{1,0:T(8,128)(2,1)S(1)}, u32[]{:S(2)}, u32[]{:S(2)}) %collective-permute-start.39) | collective-permute-done | bytes 156704 | tf_op jit(solution)/shard_map/ppermute | solution.py:197
  493.5 8.9 %collective-permute-done.46 = bf16[272,1088]{1,0:T(8,128)(2,1)} collective-permute-done((bf16[272,1088]{1,0:T(8,128)(2,1)}, bf16[272,1088]{1,0:T(8,128)(2,1)}, u32[]{:S(2)}, u32[]{:S(2)}) %collective-permute-start.46) | collective-permute-done | bytes 591904 | tf_op jit(solution)/shard_map/ppermute | solution.py:205
  (399 shorter events, 286.7 us)
Async XLA Ops:
  7.2 108.6 %all-gather.3.cloned.1.call-start = ((), (), s32[]{:S(2)}) async-start(), calls=%async_computation.1 | async-start | bytes 1566720 | tf_op jit(solution)/shard_map/all_gather | solution.py:221
  44.3 35.8 %collective-permute-start.5 = (bf16[4,144,1152]{2,1,0:T(8,128)(2,1)}, bf16[4,144,1152]{2,1,0:T(8,128)(2,1)}, u32[]{:S(2)}, u32[]{:S(2)}) collective-permute-start(bf16[4,144,1152]{2,1,0:T(8,128)(2,1)} %pad_maximum_fusion.4.refs_0_), channel_id=1, source_target_pairs={{0,4},{4,0},{8,12},{12,8},{16,20},{20,16},{24,28},{28,24},{1,5},{5... | collective-permute-start | bytes 3981320 | tf_op jit(solution)/shard_map/ppermute | solution.py:202
  45.9 169.7 %all-gather.5.cloned.1.call-start = ((), (), s32[]{:S(2)}) async-start(), calls=%async_computation.2 | async-start | bytes 5640192 | tf_op jit(solution)/shard_map/all_gather | solution.py:221
  56.0 33.2 %collective-permute-start.1 = (bf16[512,1088]{0,1:T(8,128)(2,1)S(1)}, bf16[512,1088]{0,1:T(8,128)(2,1)S(1)}, u32[]{:S(2)}, u32[]{:S(2)}) collective-permute-start(bf16[512,1088]{0,1:T(8,128)(2,1)S(1)} %bitcast.237), channel_id=1, source_target_pairs={{0,1},{1,0},{2,3},{3,2},{4,5},{5,4},{6,7},{7,6},{8,9},{9,8},{10,11... | collective-permute-start | bytes 3342344 | tf_op jit(solution)/shard_map/ppermute | solution.py:208
  63.3 140.1 %collective-permute-start = (bf16[512,1088]{0,1:T(8,128)(2,1)}, bf16[512,1088]{0,1:T(8,128)(2,1)}, u32[]{:S(2)}, u32[]{:S(2)}) collective-permute-start(bf16[512,1088]{0,1:T(8,128)(2,1)} %bitcast), channel_id=1, source_target_pairs={{0,1},{1,0},{2,3},{3,2},{4,5},{5,4},{6,7},{7,6},{8,9},{9,8},{10,11... | collective-permute-start | bytes 3342344 | tf_op jit(solution)/shard_map/ppermute | solution.py:208
  82.4 37.0 %collective-permute-start.10 = (bf16[4,136,1152]{2,1,0:T(8,128)(2,1)S(1)}, bf16[4,136,1152]{2,1,0:T(8,128)(2,1)}, u32[]{:S(2)}, u32[]{:S(2)}) collective-permute-start(bf16[4,136,1152]{2,1,0:T(8,128)(2,1)S(1)} %pad_maximum_fusion.5.refs_0_), channel_id=1, source_target_pairs={{0,4},{4,0},{8,12},{12,8},{16,20},{20,16},{24,28},{28,24},{1,5},{5... | collective-permute-start | bytes 3760136 | tf_op jit(solution)/shard_map/ppermute | solution.py:202
  85.6 33.8 %collective-permute-start.9 = (bf16[2,4,136,576]{3,2,1,0:T(8,128)(2,1)}, bf16[2,4,136,576]{3,2,1,0:T(8,128)(2,1)}, u32[]{:S(2)}, u32[]{:S(2)}) collective-permute-start(bf16[2,4,136,576]{3,2,1,0:T(8,128)(2,1)} %pad_maximum_fusion.3), channel_id=1, source_target_pairs={{0,2},{2,0},{1,3},{3,1},{4,6},{6,4},{5,7},{7,5},{8,10},{10,8},{9,1... | collective-permute-start | bytes 3760136 | tf_op jit(solution)/shard_map/ppermute | solution.py:205
  89.0 397.2 %reduce-scatter.4.cloned.1.call-start = ((), (), s32[]{:S(2)}) async-start(), calls=%async_computation.3 | async-start | bytes 5640192 | tf_op jit(solution)/shard_map/reduce_scatter | solution.py:224
  118.4 46.2 %collective-permute-start.12 = (bf16[1088,576]{0,1:T(8,128)(2,1)}, bf16[1088,576]{0,1:T(8,128)(2,1)}, u32[]{:S(2)}, u32[]{:S(2)}) collective-permute-start(bf16[1088,576]{0,1:T(8,128)(2,1)} %copy.72), channel_id=1, source_target_pairs={{0,1},{1,0},{2,3},{3,2},{4,5},{5,4},{6,7},{7,6},{8,9},{9,8},{10,11... | collective-permute-start | bytes 3760136 | tf_op jit(solution)/shard_map/ppermute | solution.py:208
  122.4 57.2 %collective-permute-start.13 = (bf16[2,4,136,1152]{3,2,1,0:T(8,128)(2,1)}, bf16[2,4,136,1152]{3,2,1,0:T(8,128)(2,1)}, u32[]{:S(2)}, u32[]{:S(2)}) collective-permute-start(bf16[2,4,136,1152]{3,2,1,0:T(8,128)(2,1)} %pad_maximum_fusion.2), channel_id=1, source_target_pairs={{0,2},{2,0},{1,3},{3,1},{4,6},{6,4},{5,7},{7,5},{8,10},{10,8},{9,1... | collective-permute-start | bytes 7520264 | tf_op jit(solution)/shard_map/ppermute | solution.py:205
  232.3 30.1 %collective-permute-start.14 = (bf16[2,2,136,1152]{3,2,1,0:T(8,128)(2,1)S(1)}, bf16[2,2,136,1152]{3,2,1,0:T(8,128)(2,1)}, u32[]{:S(2)}, u32[]{:S(2)}) collective-permute-start(bf16[2,2,136,1152]{3,2,1,0:T(8,128)(2,1)S(1)} %pad_maximum_fusion.6), channel_id=1, source_target_pairs={{0,2},{2,0},{1,3},{3,1},{4,6},{6,4},{5,7},{7,5},{8,10},{10,8},{9,1... | collective-permute-start | bytes 3760136 | tf_op jit(solution)/shard_map/ppermute | solution.py:205
  262.4 33.9 %collective-permute-start.15 = (f32[1024,1088]{0,1:T(8,128)}, f32[1024,1088]{0,1:T(8,128)}, u32[]{:S(2)}, u32[]{:S(2)}) collective-permute-start(f32[1024,1088]{0,1:T(8,128)} %fusion.92), channel_id=1, source_target_pairs={{0,1},{1,0},{2,3},{3,2},{4,5},{5,4},{6,7},{7,6},{8,9},{9,8},{10,11... | collective-permute-start | bytes 13369352 | tf_op jit(solution)/shard_map/ppermute | solution.py:208
  277.5 44.0 %collective-permute-start.18 = (bf16[2,2,136,1152]{3,2,1,0:T(8,128)(2,1)}, bf16[2,2,136,1152]{3,2,1,0:T(8,128)(2,1)}, u32[]{:S(2)}, u32[]{:S(2)}) collective-permute-start(bf16[2,2,136,1152]{3,2,1,0:T(8,128)(2,1)} %pad_maximum_fusion.7), channel_id=1, source_target_pairs={{0,2},{2,0},{1,3},{3,1},{4,6},{6,4},{5,7},{7,5},{8,10},{10,8},{9,1... | collective-permute-start | bytes 3760136 | tf_op jit(solution)/shard_map/ppermute | solution.py:205
  326.2 41.1 %collective-permute-start.22 = (bf16[4,136,576]{2,1,0:T(8,128)(2,1)}, bf16[4,136,576]{2,1,0:T(8,128)(2,1)}, u32[]{:S(2)}, u32[]{:S(2)}) collective-permute-start(bf16[4,136,576]{2,1,0:T(8,128)(2,1)} %dynamic-slice_bitcast_fusion.2), channel_id=1, source_target_pairs={{0,4},{4,0},{8,12},{12,8},{16,20},{20,16},{24,28},{28,24},{1,5},{5... | collective-permute-start | bytes 1880072 | tf_op jit(solution)/shard_map/ppermute | solution.py:202
  328.8 37.5 %collective-permute-start.20 = (bf16[136,1152]{1,0:T(8,128)(2,1)}, bf16[136,1152]{1,0:T(8,128)(2,1)}, u32[]{:S(2)}, u32[]{:S(2)}) collective-permute-start(bf16[136,1152]{1,0:T(8,128)(2,1)} %get-tuple-element.255), channel_id=1, source_target_pairs={{0,8},{4,12},{8,16},{12,20},{16,24},{20,28},{24,0},{28,4},{1,9},{5... | collective-permute-start | bytes 940040 | tf_op jit(solution)/shard_map/ppermute | solution.py:197
  335.9 31.4 %collective-permute-start.21 = (bf16[136,1152]{1,0:T(8,128)(2,1)}, bf16[136,1152]{1,0:T(8,128)(2,1)}, u32[]{:S(2)}, u32[]{:S(2)}) collective-permute-start(bf16[136,1152]{1,0:T(8,128)(2,1)} %get-tuple-element.254), channel_id=1, source_target_pairs={{0,16},{4,20},{8,24},{12,28},{16,0},{20,4},{24,8},{28,12},{1,17},{... | collective-permute-start | bytes 940040 | tf_op jit(solution)/shard_map/ppermute | solution.py:197
  387.2 36.7 %collective-permute-start.23 = (f32[512,1088]{0,1:T(8,128)}, f32[512,1088]{0,1:T(8,128)}, u32[]{:S(2)}, u32[]{:S(2)}) collective-permute-start(f32[512,1088]{0,1:T(8,128)} %constant_dynamic-slice_fusion.8), channel_id=1, source_target_pairs={{0,1},{1,0},{2,3},{3,2},{4,5},{5,4},{6,7},{7,6},{8,9},{9,8},{10,11... | collective-permute-start | bytes 6684680 | tf_op jit(solution)/shard_map/ppermute | solution.py:208
  392.2 30.6 %collective-permute-start.27 = (bf16[136,576]{1,0:T(8,128)(2,1)}, bf16[136,576]{1,0:T(8,128)(2,1)S(1)}, u32[]{:S(2)}, u32[]{:S(2)}) collective-permute-start(bf16[136,576]{1,0:T(8,128)(2,1)} %get-tuple-element.253), channel_id=1, source_target_pairs={{0,8},{4,12},{8,16},{12,20},{16,24},{20,28},{24,0},{28,4},{1,9},{5... | collective-permute-start | bytes 470024 | tf_op jit(solution)/shard_map/ppermute | solution.py:197
  398.8 32.0 %collective-permute-start.28 = (bf16[136,576]{1,0:T(8,128)(2,1)}, bf16[136,576]{1,0:T(8,128)(2,1)}, u32[]{:S(2)}, u32[]{:S(2)}) collective-permute-start(bf16[136,576]{1,0:T(8,128)(2,1)} %get-tuple-element.252), channel_id=1, source_target_pairs={{0,16},{4,20},{8,24},{12,28},{16,0},{20,4},{24,8},{28,12},{1,17},{... | collective-permute-start | bytes 470024 | tf_op jit(solution)/shard_map/ppermute | solution.py:197
  404.7 31.4 %collective-permute-start.24 = (bf16[1088,576]{0,1:T(8,128)(2,1)}, bf16[1088,576]{0,1:T(8,128)(2,1)}, u32[]{:S(2)}, u32[]{:S(2)}) collective-permute-start(bf16[1088,576]{0,1:T(8,128)(2,1)} %convolution_convert_fusion.4), channel_id=1, source_target_pairs={{0,2},{2,0},{1,3},{3,1},{4,6},{6,4},{5,7},{7,5},{8,10},{10,8},{9,1... | collective-permute-start | bytes 3760136 | tf_op jit(solution)/shard_map/ppermute | solution.py:205
  438.7 35.2 %collective-permute-start.37 = (bf16[136,1728]{1,0:T(8,128)(2,1)S(1)}, bf16[136,1728]{1,0:T(8,128)(2,1)S(1)}, u32[]{:S(2)}, u32[]{:S(2)}) collective-permute-start(bf16[136,1728]{1,0:T(8,128)(2,1)S(1)} %pad_maximum_fusion.9), channel_id=1, source_target_pairs={{0,2},{2,0},{1,3},{3,1},{4,6},{6,4},{5,7},{7,5},{8,10},{10,8},{9,1... | collective-permute-start | bytes 1410056 | tf_op jit(solution)/shard_map/ppermute | solution.py:205
  467.5 65.1 %collective-permute-start.32 = (f32[4,1,1632]{2,1,0:T(1,128)}, f32[4,1,1632]{2,1,0:T(1,128)}, u32[]{:S(2)}, u32[]{:S(2)}) collective-permute-start(f32[4,1,1632]{2,1,0:T(1,128)} %dynamic-slice_bitcast_fusion.5), channel_id=1, source_target_pairs={{0,4},{4,0},{8,12},{12,8},{16,20},{20,16},{24,28},{28,24},{1,5},{5... | collective-permute-start | bytes 78344 | tf_op jit(solution)/shard_map/ppermute | solution.py:202
  482.2 48.5 %collective-permute-start.41 = (bf16[136,576]{1,0:T(8,128)(2,1)}, bf16[136,576]{1,0:T(8,128)(2,1)}, u32[]{:S(2)}, u32[]{:S(2)}) collective-permute-start(bf16[136,576]{1,0:T(8,128)(2,1)} %get-tuple-element.247), channel_id=1, source_target_pairs={{0,8},{4,12},{8,16},{12,20},{16,24},{20,28},{24,0},{28,4},{1,9},{5... | collective-permute-start | bytes 470024 | tf_op jit(solution)/shard_map/ppermute | solution.py:197
  488.7 42.0 %collective-permute-start.42 = (bf16[136,576]{1,0:T(8,128)(2,1)}, bf16[136,576]{1,0:T(8,128)(2,1)}, u32[]{:S(2)}, u32[]{:S(2)}) collective-permute-start(bf16[136,576]{1,0:T(8,128)(2,1)} %get-tuple-element.246), channel_id=1, source_target_pairs={{0,16},{4,20},{8,24},{12,28},{16,0},{20,4},{24,8},{28,12},{1,17},{... | collective-permute-start | bytes 470024 | tf_op jit(solution)/shard_map/ppermute | solution.py:197
  (96 other events, 1261.4 us)
Sparse Core Ops, SparseCore 0:
  46.0 69.7 all-gather.2
  118.6 81.8 all-gather.4
  286.6 135.0 reduce-scatter.3
where the time goes:
time: 566 us; the launch traced here: 555 us
  local copies, waits for them, and re-layouts  124 us (22%)
  waiting for transfers between devices  106 us (19%)
  matrix products  93.7 us (17%)
  other arithmetic  91 us (16%)
  starting transfers between devices  70.7 us (12%)
  Pallas kernels  54.7 us (10%)
  between operations  15.6 us (3%)
    dot_general x14, matrix products, product(): lax.dot_general(left, right, (((left_dim,), (right_dim,)), ((), ())), pre...  93.7 us
    ppermute x21, starting transfers between devices, far_shift(): return lax.ppermute(array, 'fsdp', pairs)  50 us
    ppermute x21, waiting for transfers between devices, far_shift(): return lax.ppermute(array, 'fsdp', pairs)  43.3 us
    ppermute x10, waiting for transfers between devices, swap_rep(): return lax.ppermute(array, 'rep', [(0, 1), (1, 0)])  29.2 us
    unnamed x132, local copies, waits for them, and re-layouts  26.1 us
    all_gather x2, waiting for transfers between devices, gather_all(): return lax.all_gather(piece, 'fsdp', axis=0, tiled=True)  24.9 us
    pallas_call x1, Pallas kernels, attend_back(): pl.pallas_call(bwd_kernel, out_shape=jax.ShapeDtypeStruct((3, heads, HD,...  22.7 us
    pallas_call x1, Pallas kernels, attend(): pl.pallas_call(fwd_kernel, out_shape=(jax.ShapeDtypeStruct((heads, HD, to...  22 us
  transfers between devices with their start and end apart: 54, of which 16 were waited for; matrix products, arithmetic and copies ran while one was open for 48% of the time, Pallas kernels for 10%

commit v1 on v0

--- a/solution.py
+++ b/solution.py
@@ -174,6 +174,79 @@
         ),
         name="assemble",
     )(info, *arrays)
+
+
+def finish_pair(info, own, other, count, up_wide, skip):
+    rows, total = own[0].shape
+    wide = total - up_wide
+    slab = (up_wide + up_wide // 128 * 128 - 128) // count
+    up_skip = slab * count - up_wide
+
+    def kernel(info_ref, a_ref, b_ref, c_ref, d_ref, up_ref, out_ref):
+        flip, turn = info_ref[0] == 1, info_ref[1] == 1
+
+        def both(x, y, take):
+            x, y = x[...].astype(F32), y[...].astype(F32)
+            low, high = jnp.where(flip, y, x), jnp.where(flip, x, y)
+            ups = jnp.concatenate([low[:, :up_skip], high[:, :up_wide]], axis=1)
+            return ups, x[:, up_wide:] + y[:, up_wide:]
+
+        own_up, own_out = both(a_ref, b_ref, 0)
+        other_up, other_out = both(c_ref, d_ref, 1)
+        up_low, up_high = jnp.where(turn, other_up, own_up), jnp.where(turn, own_up, other_up)
+        for p in range(count):
+            at = slice(p * slab, (p + 1) * slab)
+            up_ref[:, 2 * p * slab : (2 * p + 1) * slab] = up_low[:, at]
+            up_ref[:, (2 * p + 1) * slab : (2 * p + 2) * slab] = up_high[:, at]
+        out_ref[:, :skip] = jnp.where(turn, other_out, own_out)[:, :skip]
+        out_ref[:, skip:] = jnp.where(turn, own_out, other_out)
+
+    return pl.pallas_call(
+        kernel,
+        out_shape=(
+            jax.ShapeDtypeStruct((rows, 2 * slab * count), F32),
+            jax.ShapeDtypeStruct((rows, skip + wide), F32),
+        ),
+        grid_spec=pltpu.PrefetchScalarGridSpec(
+            num_scalar_prefetch=1,
+            grid=(1,),
+            in_specs=[pl.BlockSpec((rows, total), lambda i, s: (0, 0))] * 4,
+            out_specs=(
+                pl.BlockSpec((rows, 2 * slab * count), lambda i, s: (0, 0)),
+                pl.BlockSpec((rows, skip + wide), lambda i, s: (0, 0)),
+            ),
+        ),
+        cost_estimate=pl.CostEstimate(
+            flops=0, bytes_accessed=8 * rows * total + 8 * rows * slab * count, transcendentals=0
+        ),
+        name="finish_pair",
+    )(info, *own, *other)
+
+
+def finish_down(info, own, other):
+    rows, width = own[0].shape
+
+    def kernel(info_ref, a_ref, b_ref, c_ref, d_ref, out_ref):
+        turn = info_ref[1] == 1
+        mine = a_ref[...].astype(F32) + b_ref[...].astype(F32)
+        theirs = c_ref[...].astype(F32) + d_ref[...].astype(F32)
+        out_ref[:rows] = jnp.where(turn, theirs, mine)
+        out_ref[rows:] = jnp.where(turn, mine, theirs)
+
+    return pl.pallas_call(
+        kernel,
+        out_shape=jax.ShapeDtypeStruct((2 * rows, width), F32),
+        grid_spec=pltpu.PrefetchScalarGridSpec(
+            num_scalar_prefetch=1,
+            grid=(1,),
+            in_specs=[pl.BlockSpec((rows, width), lambda i, s: (0, 0))] * 4,
+            out_specs=pl.BlockSpec((2 * rows, width), lambda i, s: (0, 0)),
+        ),
+        cost_estimate=pl.CostEstimate(
+            flops=0, bytes_accessed=16 * rows * width, transcendentals=0
+        ),
+        name="finish_down",
+    )(info, *own, *other)
 
 
 class Grid:
@@ -313,7 +386,6 @@
 
     small = [ln1_gain, ln1_bias, b_qv, b_out, ln2_gain, ln2_bias, b_up, b_down]
     sizes = [v.shape[0] for v in small]
-    vec = jnp.concatenate(small)
 
     def section(k):
         low = w_qkv[:, k * width : k * width + wide]
@@ -329,8 +401,7 @@
     if grid.split:
         far = grid.far
         mine = jnp.where(lead, w_q, w_v)
-        tail_rows = -(-vec.shape[0] // (2 * wide))
-        tail = jnp.pad(vec, (0, 8 * 2 * wide - vec.shape[0])).reshape(8, 2 * wide)
+        tail = jnp.stack([jnp.pad(v, (0, 2 * wide - v.shape[0])) for v in small])
         lines = grid.lines(
             jnp.concatenate([jnp.concatenate([mine, w_k], axis=1), tail], axis=0)
         )
@@ -347,12 +418,29 @@
         )
         up_near = jnp.stack(up_lines)
         up_next = grid.near_shift(up_near, 1)
-        qkv_near, qkv_next, qkv_other, up_near, up_next = hold(
-            (qkv_near, qkv_next, qkv_other, up_near, up_next)
-        )
         spots = jnp.stack(
             grid.spots() + [up_skip * y, (up_wide - up_skip) * (1 - y), up_wide * (1 - y)]
         ).astype(jnp.int32)
+        tails = jnp.concatenate([qkv_near[:, part:, : max(sizes)], qkv_next[:, part:, : max(sizes)]])
+        chosen = spots[None, :count, None, None] == jnp.arange(count)[:, None, None, None]
+        tails = jnp.sum(jnp.where(chosen, tails[None].astype(F32), 0.0), axis=1)
+        small_full = [tails[:, i, :size].reshape(-1) for i, size in enumerate(sizes)]
+    else:
+        small_full = [grid.gather_all(v).astype(F32) for v in small]
+        half_out = grid.gather_all(out_own)
+        full_up = grid.gather_all(up_own)
+        full_down = grid.gather_all(down_own)
+    gain_one, shift_one, bias_qv, bias_out, gain_two, shift_two, bias_up, bias_down = small_full
+
+    all_tokens = both(own_tokens, grid.swap_ctx(own_tokens))
+    all_cot = both(own_cot, grid.swap_ctx(own_cot))
+    inputs = all_tokens.astype(F32)
+    scaled_one, _ = moments(inputs)
+    normed = (scaled_one * gain_one + shift_one).astype(BF)
+    if grid.split:
+        qkv_near, qkv_next, qkv_other, up_near, up_next, normed = hold(
+            (qkv_near, qkv_next, qkv_other, up_near, up_next, normed)
+        )
         full_qkv = assemble(
             spots,
             [qkv_near, qkv_next, qkv_other],
@@ -360,30 +448,11 @@
             + [(2, (i // far, i % far), i, 0, 2 * wide, wide) for i in range(count)],
             (count, part, 3 * wide),
         )
-        tails = jnp.concatenate([qkv_near, qkv_next])[:, part : part + tail_rows]
-        chosen = spots[None, :count, None] == jnp.arange(count)[:, None, None]
-        vec_full = jnp.sum(
-            jnp.where(chosen, tails.reshape(1, count, -1).astype(F32), 0.0), axis=1
-        )
         up_other = grid.swap_rep(jnp.stack([up_near, up_next]))
     else:
         full_qkv = grid.gather_all(jnp.concatenate([w_q, w_k, w_v], axis=1))
-        vec_full = grid.gather_all(vec.reshape(1, -1)).astype(F32)
-        half_out = grid.gather_all(out_own)
-        full_up = grid.gather_all(up_own)
-        full_down = grid.gather_all(down_own)
     full_qkv = full_qkv.reshape(width, 3 * wide)
-    small_full, at = [], 0
-    for size in sizes:
-        small_full.append(vec_full[:, at : at + size].reshape(-1))
-        at += size
-    gain_one, shift_one, bias_qv, bias_out, gain_two, shift_two, bias_up, bias_down = small_full
-
-    all_tokens = both(own_tokens, grid.swap_ctx(own_tokens))
-    all_cot = both(own_cot, grid.swap_ctx(own_cot))
-    inputs = all_tokens.astype(F32)
-    scaled_one, _ = moments(inputs)
-    normed = (scaled_one * gain_one + shift_one).astype(BF)
+
     bias_q = lax.dynamic_slice(bias_qv, (skip * c,), (wide,))
     bias_v = lax.dynamic_slice(bias_qv, (width + skip * c,), (wide,))
     bias_row = jnp.concatenate(
@@ -451,19 +520,19 @@
         own_down = grid.scatter_all(grad_down)
         grad_up = product(hidden_in, grad_pre, 0, 0).astype(BF)
     grad_hidden = product(grad_pre, full_up, 1, 1)
-    if grid.split:
-        grad_hidden, up_mine, up_sent[0], activated = hold(
-            (grad_hidden, up_mine, up_sent[0], activated)
+    partial_down = product(activated, full_down, 1, 0)
+    result = own_rows(partial_down) + grid.swap_ctx(other_rows(partial_down))
+    block_out = (own_rows(middle) + result + bias_down).astype(BF).reshape(seqs, rows, width)
+    grad_hidden = grad_hidden + grid.swap_ctx(grad_hidden)
+    if grid.split:
+        grad_hidden, up_mine, up_sent[0], block_out = hold(
+            (grad_hidden, up_mine, up_sent[0], block_out)
         )
         merge = lambda i: (
             grid.pick_lines(up_mine, groups[i]).astype(F32) + up_sent[i].astype(F32)
         ).astype(BF)
         up_cubes = [merge(0)]
         up_near = [grid.near_send(up_cubes[0])]
-    partial_down = product(activated, full_down, 1, 0)
-    result = own_rows(partial_down) + grid.swap_ctx(other_rows(partial_down))
-    block_out = (own_rows(middle) + result + bias_down).astype(BF).reshape(seqs, rows, width)
-    grad_hidden = grad_hidden + grid.swap_ctx(grad_hidden)
     grad_middle = all_cot.astype(F32) + norm_backward(grad_hidden, scaled_two, inverse_two, gain_two)
     grad_branch = grad_middle.astype(BF)
     if grid.split:
@@ -498,25 +567,35 @@
         ]
     grad_project = grad_cube.reshape(3 * wide, total_len)
     qkv_sent = product(normed, grad_project[2 * wide :], 0, 1).astype(BF)
-    qkv_mine = product(normed, grad_project[: 2 * wide], 0, 1).astype(BF)
-    if grid.split:
-        qkv_sent, qkv_mine, grad_project = hold((qkv_sent, qkv_mine, grad_project))
+    if grid.split:
+        qkv_keys = product(normed, grad_project[wide : 2 * wide], 0, 1).astype(BF)
+        qkv_mine = product(normed, grad_project[:wide], 0, 1).astype(BF)
+    else:
+        qkv_mine = product(normed, grad_project[: 2 * wide], 0, 1).astype(BF)
+    if grid.split:
+        qkv_sent, qkv_mine, qkv_keys, grad_project = hold(
+            (qkv_sent, qkv_mine, qkv_keys, grad_project)
+        )
         qkv_sent = grid.swap_rep(qkv_sent)
-        key_cube = rows_cube(qkv_mine[:, wide:])
+        key_cube = rows_cube(qkv_keys)
         key_near = grid.near_send(key_cube)
     grad_normed = product(grad_project, full_qkv, 0, 1)
+    if grid.split:
+        qkv_sent, qkv_mine, key_near, key_cube, grad_normed = hold(
+            (qkv_sent, qkv_mine, key_near, key_cube, grad_normed)
+        )
+        low = qkv_mine.astype(F32) + qkv_sent.astype(F32)
+        low_cube = rows_cube(low.astype(BF))
+        low_near = grid.near_send(low_cube)
     own_grad = own_rows(grad_normed) + grid.swap_ctx(other_rows(grad_normed))
     own_scaled, own_inverse = moments(own_tokens.astype(F32))
     grad_tokens = own_rows(grad_middle) + norm_backward(own_grad, own_scaled, own_inverse, gain_one)
     grad_tokens = grad_tokens.reshape(seqs, rows, width)
 
     if grid.split:
-        qkv_sent, qkv_mine, key_near, key_cube, up_far, out_far, own_grad = hold(
-            (qkv_sent, qkv_mine, key_near, key_cube, up_far, out_far, own_grad)
-        )
-        low = qkv_mine[:, :wide].astype(F32) + qkv_sent.astype(F32)
-        low_cube = rows_cube(low.astype(BF))
-        low_near = grid.near_send(low_cube)
+        low_near, low_cube, key_near, key_cube, up_far, out_far, own_grad = hold(
+            (low_near, low_cube, key_near, key_cube, up_far, out_far, own_grad)
+        )
         key_far = [
             grid.far_shift(grid.near_sum(key_cube, key_near, k).astype(BF), k)
             for k in range(1, far)
@@ -528,46 +607,51 @@
         for extra in out_far:
             out_total += extra.astype(F32)
         pair = jnp.concatenate([up_total.astype(BF), out_total.astype(BF)], axis=1)
-        pair_other = grid.swap_rep(pair)
-        low_near, low_cube, pair, pair_other, key_far = hold(
-            (low_near, low_cube, pair, pair_other, key_far)
-        )
         low_far = [
             grid.far_shift(grid.near_sum(low_cube, low_near, k).astype(BF), k)
             for k in range(1, far)
         ]
-    own_down = grid.sum_rep(own_down).astype(BF)
-    other_down = grid.swap_ctx(own_down)
-    out_down = jnp.where(
-        first,
-        jnp.concatenate([own_down, other_down], axis=0),
-        jnp.concatenate([other_down, own_down], axis=0),
-    ).astype(F32)
-
-    if grid.split:
-        mine, other = pair[:, :up_wide], pair_other[:, :up_wide]
-        own_up = jnp.concatenate(
-            [jnp.where(lead, mine, other)[:, :up_skip], jnp.where(lead, other, mine)], axis=1
+        pair_other = grid.swap_rep(pair)
+        places = jnp.stack([y, c]).astype(jnp.int32)
+        out_up, out_wout = finish_pair(
+            places,
+            (pair, pair_other),
+            (grid.swap_ctx(pair), grid.swap_ctx(pair_other)),
+            count,
+            up_wide,
+            skip,
+        )
+        down_other = grid.swap_rep(own_down)
+        out_down = finish_down(
+            places,
+            (own_down, down_other),
+            (grid.swap_ctx(own_down), grid.swap_ctx(down_other)),
         )
     else:
+        own_down = grid.sum_rep(own_down).astype(BF)
+        other_down = grid.swap_ctx(own_down)
+        out_down = jnp.where(
+            first,
+            jnp.concatenate([own_down, other_down], axis=0),
+            jnp.concatenate([other_down, own_down], axis=0),
+        ).astype(F32)
         own_up = grid.sum_rep(grid.scatter_all(grad_up)).astype(BF)
-    other_up = grid.swap_ctx(own_up)
-    weave = lambda a, b: jnp.stack(
-        [a.reshape(part, count, slab), b.reshape(part, count, slab)], axis=2
-    ).reshape(part, ff)
-    out_up = weave(
-        jnp.where(first, own_up, other_up), jnp.where(first, other_up, own_up)
-    ).astype(F32)
-
-    if grid.split:
-        own_wout = (pair[:, up_wide:].astype(F32) + pair_other[:, up_wide:].astype(F32)).astype(BF)
-    else:
+        other_up = grid.swap_ctx(own_up)
+        weave = lambda a, b: jnp.stack(
+            [a.reshape(part, count, slab), b.reshape(part, count, slab)], axis=2
+        ).reshape(part, ff)
+        out_up = weave(
+            jnp.where(first, own_up, other_up), jnp.where(first, other_up, own_up)
+        ).astype(F32)
         own_wout = grid.sum_rep(grid.scatter_all(grad_wout)).astype(BF)
-    other_wout = grid.swap_ctx(own_wout)
-    out_wout = jnp.concatenate(
-        [jnp.where(first, own_wout, other_wout)[:, :skip], jnp.where(first, other_wout, own_wout)],
-        axis=1,
-    ).astype(F32)
+        other_wout = grid.swap_ctx(own_wout)
+        out_wout = jnp.concatenate(
+            [
+                jnp.where(first, own_wout, other_wout)[:, :skip],
+                jnp.where(first, other_wout, own_wout),
+            ],
+            axis=1,
+        ).astype(F32)
 
     if grid.split:
         keys = grid.near_sum(key_cube, key_near, 0)

time: 566 us -> 536 us (0.947)
  local copies, waits for them, and re-layouts: 124 us -> 83.5 us
  waiting for transfers between devices: 106 us -> 129 us
  starting transfers between devices: 70.7 us -> 57.3 us
  other arithmetic: 91 us -> 80 us
  Pallas kernels: 54.7 us -> 62.9 us
    ppermute x8, waiting for transfers between devices: 6.85 us -> 33.1 us  [near_shift(): return lax.ppermute(array, 'fsdp', pairs)]
    unnamed x132 -> x104, local copies, waits for them, and re-layouts: 26.1 us -> 7.73 us
    all_gather x2, waiting for transfers between devices: 24.9 us -> 11.4 us  [gather_all(): return lax.all_gather(piece, 'fsdp', axis=0, tiled=True)]
    ppermute x21, starting transfers between devices: 50 us -> 36.5 us  [far_shift(): return lax.ppermute(array, 'fsdp', pairs)]
    convert_element_type x3 -> x0, local copies, waits for them, and re-layouts: 10.6 us -> none  [the longest x2 9.51 us: shards(): out_up = weave(jnp.where(first, own_up, other_up), jnp.where(first, other...]
    pallas_call x0 -> x2, Pallas kernels: none -> 8.57 us  [the longest x1 4.41 us: finish_pair(): pl.pallas_call(kernel, out_shape=(jax.ShapeDtypeStruct((rows, 2 * slab *...]
    ppermute x10, waiting for transfers between devices: 29.2 us -> 35.5 us  [swap_rep(): return lax.ppermute(array, 'rep', [(0, 1), (1, 0)])]
    another operation x4 -> x11, local copies, waits for them, and re-layouts: 6.11 us -> 0.15 us  [the longest x1 0.08 us: shards(): tails[:, i, :size].reshape(-1)]
  transfers between devices with their start and end apart: 54 -> 55, of which waited for: 16 -> 20; matrix products, arithmetic and copies ran while one was open for 48% -> 43% of each run, Pallas kernels for 10% -> 12%
where the time goes in v1:
time: 536 us; the launch traced here: 527 us
  waiting for transfers between devices  129 us (24%)
  matrix products  98.5 us (18%)
  local copies, waits for them, and re-layouts  83.5 us (16%)
  other arithmetic  80 us (15%)
  Pallas kernels  62.9 us (12%)
  starting transfers between devices  57.3 us (11%)
  between operations  15.9 us (3%)
    dot_general x15, matrix products, product(): lax.dot_general(left, right, (((left_dim,), (right_dim,)), ((), ())), pre...  98.5 us
    ppermute x21, waiting for transfers between devices, far_shift(): return lax.ppermute(array, 'fsdp', pairs)  47.4 us
    ppermute x21, starting transfers between devices, far_shift(): return lax.ppermute(array, 'fsdp', pairs)  36.5 us
    ppermute x10, waiting for transfers between devices, swap_rep(): return lax.ppermute(array, 'rep', [(0, 1), (1, 0)])  35.5 us
    ppermute x8, waiting for transfers between devices, near_shift(): return lax.ppermute(array, 'fsdp', pairs)  33.1 us
    pallas_call x1, Pallas kernels, attend_back(): pl.pallas_call(bwd_kernel, out_shape=jax.ShapeDtypeStruct((3, heads, HD,...  22.3 us
    pallas_call x1, Pallas kernels, attend(): pl.pallas_call(fwd_kernel, out_shape=(jax.ShapeDtypeStruct((heads, HD, to...  22 us
    all_gather x2, waiting for transfers between devices, gather_all(): return lax.all_gather(piece, 'fsdp', axis=0, tiled=True)  11.4 us
  transfers between devices with their start and end apart: 55, of which 20 were waited for; matrix products, arithmetic and copies ran while one was open for 43% of the time, Pallas kernels for 12%

profile of v1, /device:TPU:0, one launch (start us, length us, event | category | flops | bytes accessed | tf_op | source)
XLA Modules:
  0.0 527.0 jit_solution(8372167823864677762)
XLA Ops:
  21.7 6.4 %reshape.404 = bf16[136,8,2,272]{3,2,1,0:T(2,128)(2,1)} reshape(bf16[136,4352]{1,0:T(8,128)(2,1)} %param.25) | data formatting | bytes 2367488 | tf_op jit(solution)/shard_map/reshape | solution.py:397
  28.0 6.7 %dynamic-slice_reduce_fusion = bf16[136,8,272]{2,1,0:T(8,128)(2,1)S(1)} fusion(bf16[136,8,2,272]{3,2,1,0:T(2,128)(2,1)} %reshape.404, s32[]{:T(128)S(6)} %select_n.385), kind=kLoop, calls=%fused_computation.67 | loop fusion | bytes 1183748 | tf_op jit(solution)/shard_map/jit(dynamic_index_in_dim)/dynamic_slice | solution.py:398
  49.5 7.6 %collective-permute-start.6 = (bf16[136,1152]{1,0:T(8,128)(2,1)S(1)}, bf16[136,1152]{1,0:T(8,128)(2,1)S(1)}, u32[]{:S(2)}, u32[]{:S(2)}) collective-permute-start(bf16[136,1152]{1,0:T(8,128)(2,1)S(1)} %copy-done.22), channel_id=1, source_target_pairs={{0,8},{4,12},{8,16},{12,20},{16,24},{20,28},{24,0},{28,4},{1,9},{5... | collective-permute-start | bytes 940040 | tf_op jit(solution)/shard_map/ppermute | solution.py:270
  61.4 10.1 %collective-permute-done.6 = bf16[136,1152]{1,0:T(8,128)(2,1)S(1)} collective-permute-done((bf16[136,1152]{1,0:T(8,128)(2,1)S(1)}, bf16[136,1152]{1,0:T(8,128)(2,1)S(1)}, u32[]{:S(2)}, u32[]{:S(2)}) %collective-permute-start.6) | collective-permute-done | bytes 313376 | tf_op jit(solution)/shard_map/ppermute | solution.py:270
  71.5 13.0 %collective-permute-done.7 = bf16[136,1152]{1,0:T(8,128)(2,1)S(1)} collective-permute-done((bf16[136,1152]{1,0:T(8,128)(2,1)S(1)}, bf16[136,1152]{1,0:T(8,128)(2,1)S(1)}, u32[]{:S(2)}, u32[]{:S(2)}) %collective-permute-start.7) | collective-permute-done | bytes 313376 | tf_op jit(solution)/shard_map/ppermute | solution.py:270
  99.8 11.4 %all-gather.3.cloned.1.call-done = bf16[1088,576]{1,0:T(8,128)(2,1)} async-done(((bf16[136,576]{1,0:T(8,128)(2,1)}), bf16[1088,576]{1,0:T(8,128)(2,1)}) %all-gather.3.cloned.1.call-update) | async-done | bytes 1253392 | tf_op jit(solution)/shard_map/all_gather | solution.py:294
  113.8 13.7 %collective-permute-done.10.refs_1_ = bf16[4,136,1152]{2,1,0:T(8,128)(2,1)} collective-permute-done((bf16[4,136,1152]{2,1,0:T(8,128)(2,1)S(1)}, bf16[4,136,1152]{2,1,0:T(8,128)(2,1)}, u32[]{:S(2)}, u32[]{:S(2)}) %collective-permute-start.10) | collective-permute-done | bytes 1253408 | tf_op jit(solution)/shard_map/ppermute | solution.py:275
  136.8 9.4 %add_convert_fusion = bf16[1728,1024]{1,0:T(8,128)(2,1)} fusion(bf16[1088,1728]{1,0:T(8,128)(2,1)} %bitcast.261, bf16[1024,1088]{0,1:T(8,128)(2,1)} %fusion.11, f32[1728]{0:T(1024)S(1)} %concatenate.65), kind=kOutput, calls=%fused_computation.14 | convolution fusion | flops 3853910016 | bytes 9534208 | tf_op jit(solution)/shard_map/dot_general | solution.py:112
  146.3 22.0 %attend.1 = (bf16[9,64,1024]{2,1,0:T(8,128)(2,1)}, f32[9,1,1024]{2,1,0:T(1,128)}) custom-call(s32[4]{0:T(128)} %pad_add_fusion.info, bf16[27,64,1024]{2,1,0:T(8,128)(2,1)} %bitcast.288, bf16[27,64,1024]{2,1,0:T(8,128)(2,1)} %bitcast.289, bf16[27,64,1024]{2,1,0:T(8,128)(2,1)} %bitcast.290), custom_call_target="tpu_custom_call" | custom-call | flops 2415919104 | bytes 4718592 | tf_op jit(solution)/shard_map/attend/pallas_call | solution.py:82
  178.6 7.0 %fusion.7 = f32[1024,1088]{0,1:T(8,128)} fusion(bf16[1088,512]{1,0:T(8,128)(2,1)S(1)} %slice_select_fusion, bf16[1088,576]{1,0:T(8,128)(2,1)S(1)} %broadcast_select_fusion, f32[1088]{0:T(1024)S(1)} %copy-done.45, bf16[512,1024]{1,0:T(8,128)(2,1)S(1)} %slice.221, bf16[576,1024]{1,0:T(8,128)(2,1)S(1)} %bitcast.278, bf16[512,1024]{1,0:T(8,128)(2,1)S(1)} %bitcast.275, ...), kind=kOutput, calls=%fused_computation.22 | convolution fusion | flops 2452439040 | bytes 13512961 | tf_op jit(solution)/shard_map/dot_general | solution.py:112
  200.7 9.3 %multiply_convert_fusion.1 = (bf16[1024,2176]{1,0:T(8,128)(2,1)S(1)}, f32[1024,2176]{1,0:T(8,128)}) fusion(f32[2176]{0:T(1024)S(1)} %add.583, bf16[1024,1088]{0,1:T(8,128)(2,1)S(1)} %add_convert_fusion.1, bf16[1088,2176]{1,0:T(8,128)(2,1)S(1)} %bitcast.257), kind=kOutput, calls=%fused_computation.9 | convolution fusion | flops 4861984768 | bytes 20341248 | tf_op jit(solution)/shard_map/dot_general | solution.py:112
  212.0 9.6 %convolution_convert_fusion = bf16[2176,1088]{1,0:T(8,128)(2,1)} fusion(bf16[1024,2176]{1,0:T(8,128)(2,1)S(1)} %get-tuple-element.224, bf16[512,1088]{0,1:T(8,128)(2,1)} %collective-permute-done, bf16[512,1088]{0,1:T(8,128)(2,1)S(1)} %bitcast.271, pred[]{:T(512)S(6)} %eq.72), kind=kOutput, calls=%fused_computation.1 | convolution fusion | flops 4861009920 | bytes 11419649 | tf_op jit(solution)/shard_map/dot_general | solution.py:112
  221.6 11.5 %convert_reduce_fusion = (f32[2176]{0:T(1024)S(1)}, bf16[1024,2176]{1,0:T(8,128)(2,1)S(1)}) fusion(f32[1024,2176]{1,0:T(8,128)} %get-tuple-element.225, f32[2176]{0:T(1024)S(1)} %add.583, bf16[2176,1088]{1,0:T(8,128)(2,1)} %all-gather.5.cloned.1.call-done, bf16[512,1088]{0,1:T(8,128)(2,1)} %collective-permute-done, bf16[512,1088]{0,1:T(8,128)(2,1)S(1)} %bitcast.272, ...), kind=kOutput, calls=%fused_computation.7 | convolution fusion | flops 4892063744 | bytes 20349952 | tf_op jit(solution)/shard_map/dot_general | solution.py:112
  233.2 7.4 %fusion.86 = f32[1024,1088]{0,1:T(8,128)} fusion(bf16[1024,2176]{1,0:T(8,128)(2,1)S(1)} %get-tuple-element.227, bf16[1088,2176]{1,0:T(8,128)(2,1)S(1)} %bitcast.260), kind=kOutput, calls=%fused_computation.224 | convolution fusion | flops 4848615424 | bytes 13647872 | tf_op jit(solution)/shard_map/dot_general | solution.py:112
  241.1 9.1 %fusion.87 = f32[1024,1088]{0,1:T(8,128)S(1)} fusion(bf16[1024,2176]{1,0:T(8,128)(2,1)} %copy-done.46, bf16[2176,1088]{1,0:T(8,128)(2,1)} %all-gather.5.cloned.1.call-done), kind=kOutput, calls=%fused_computation.225 | convolution fusion | flops 4848615424 | bytes 13647872 | tf_op jit(solution)/shard_map/dot_general | solution.py:112
  279.8 11.9 %collective-permute-done.15 = bf16[2,2,136,1152]{3,2,1,0:T(8,128)(2,1)} collective-permute-done((bf16[2,2,136,1152]{3,2,1,0:T(8,128)(2,1)}, bf16[2,2,136,1152]{3,2,1,0:T(8,128)(2,1)}, u32[]{:S(2)}, u32[]{:S(2)}) %collective-permute-start.15) | collective-permute-done | bytes 1253408 | tf_op jit(solution)/shard_map/ppermute | solution.py:278
  298.3 6.4 %fusion.81 = (bf16[1024,1088]{0,1:T(8,128)(2,1)}, f32[1024,1088]{0,1:T(8,128)}, f32[1088]{0:T(1024)S(1)}) fusion(f32[1024]{0:T(1024)S(1)} %broadcast_multiply_fusion.4, f32[1024,1088]{0,1:T(8,128)S(1)} %bitcast.239, f32[1024]{0:T(1024)S(1)} %broadcast_multiply_fusion.6, f32[1024]{0:T(1024)S(1)} %broadcast_multiply_fusion.5, f32[1024,1088]{0,1:T(8,128)S(1)} %add.588, ...), kind=kLoop, calls=%fused_computation.219 | loop fusion | flops 22281152 | bytes 17850880 | tf_op jit(solution)/shard_map/convert_element_type | solution.py:537
  306.0 9.0 %collective-permute-done.17 = bf16[2,136,1152]{2,1,0:T(8,128)(2,1)} collective-permute-done((bf16[2,136,1152]{2,1,0:T(8,128)(2,1)}, bf16[2,136,1152]{2,1,0:T(8,128)(2,1)}, u32[]{:S(2)}, u32[]{:S(2)}) %collective-permute-start.17) | collective-permute-done | bytes 626720 | tf_op jit(solution)/shard_map/ppermute | solution.py:275
  337.4 22.3 %attend_back.1 = bf16[3,9,64,1024]{3,2,1,0:T(8,128)(2,1)} custom-call(s32[4]{0:T(128)} %pad_add_fusion.info, bf16[27,64,1024]{2,1,0:T(8,128)(2,1)} %bitcast.291, bf16[27,64,1024]{2,1,0:T(8,128)(2,1)} %bitcast.292, bf16[27,64,1024]{2,1,0:T(8,128)(2,1)} %bitcast.293, bf16[9,64,1024]{2,1,0:T(8,128)(2,1)} %get-tuple-element.101.o_ref, ...), custom_call_target="tpu_custom_call" | custom-call | flops 6039797760 | bytes 9437184 | tf_op jit(solution)/shard_map/attend_back/pallas_call | solution.py:96
  359.6 14.0 %collective-permute-done.21 = bf16[136,1152]{1,0:T(8,128)(2,1)} collective-permute-done((bf16[136,1152]{1,0:T(8,128)(2,1)}, bf16[136,1152]{1,0:T(8,128)(2,1)}, u32[]{:S(2)}, u32[]{:S(2)}) %collective-permute-start.21) | collective-permute-done | bytes 313376 | tf_op jit(solution)/shard_map/ppermute | solution.py:270
  391.4 7.4 %fusion.88 = f32[1024,1088]{0,1:T(8,128)S(1)} fusion(bf16[1088,1728]{1,0:T(8,128)(2,1)} %bitcast.262, bf16[1728,1024]{1,0:T(8,128)(2,1)} %bitcast.245), kind=kOutput, calls=%fused_computation.226 | convolution fusion | flops 3850371072 | bytes 11755520 | tf_op jit(solution)/shard_map/dot_general | solution.py:112
  402.7 8.2 %collective-permute-done.23 = bf16[1088,576]{0,1:T(8,128)(2,1)} collective-permute-done((bf16[1088,576]{0,1:T(8,128)(2,1)}, bf16[1088,576]{0,1:T(8,128)(2,1)}, u32[]{:S(2)}, u32[]{:S(2)}) %collective-permute-start.23) | collective-permute-done | bytes 1253408 | tf_op jit(solution)/shard_map/ppermute | solution.py:278
  441.0 6.7 %collective-permute-done.26 = bf16[4,136,576]{2,1,0:T(8,128)(2,1)} collective-permute-done((bf16[4,136,576]{2,1,0:T(8,128)(2,1)}, bf16[4,136,576]{2,1,0:T(8,128)(2,1)}, u32[]{:S(2)}, u32[]{:S(2)}) %collective-permute-start.26) | collective-permute-done | bytes 626720 | tf_op jit(solution)/shard_map/ppermute | solution.py:275
  466.8 10.2 %collective-permute-done.32 = f32[8,1632]{1,0:T(8,128)S(1)} collective-permute-done((f32[8,1632]{1,0:T(8,128)S(1)}, f32[8,1632]{1,0:T(8,128)S(1)}, u32[]{:S(2)}, u32[]{:S(2)}) %collective-permute-start.32) | collective-permute-done | bytes 52256 | tf_op jit(solution)/shard_map/ppermute | solution.py:278
  (373 shorter events, 260.8 us)
Async XLA Ops:
  7.2 104.0 %all-gather.3.cloned.1.call-start = ((), (), s32[]{:S(2)}) async-start(), calls=%async_computation.1 | async-start | bytes 1566720 | tf_op jit(solution)/shard_map/all_gather | solution.py:294
  14.6 25.9 %collective-permute-start.2 = (bf16[144,1152]{1,0:T(8,128)(2,1)S(1)}, bf16[144,1152]{1,0:T(8,128)(2,1)}, u32[]{:S(2)}, u32[]{:S(2)}) collective-permute-start(bf16[144,1152]{1,0:T(8,128)(2,1)S(1)} %concatenate.63), channel_id=1, source_target_pairs={{0,8},{4,12},{8,16},{12,20},{16,24},{20,28},{24,0},{28,4},{1,9},{5... | collective-permute-start | bytes 995336 | tf_op jit(solution)/shard_map/ppermute | solution.py:270
  17.7 24.3 %collective-permute-start.3 = (bf16[144,1152]{1,0:T(8,128)(2,1)S(1)}, bf16[144,1152]{1,0:T(8,128)(2,1)}, u32[]{:S(2)}, u32[]{:S(2)}) collective-permute-start(bf16[144,1152]{1,0:T(8,128)(2,1)S(1)} %concatenate.63), channel_id=1, source_target_pairs={{0,16},{4,20},{8,24},{12,28},{16,0},{20,4},{24,8},{28,12},{1,17},{... | collective-permute-start | bytes 995336 | tf_op jit(solution)/shard_map/ppermute | solution.py:270
  42.0 179.6 %all-gather.5.cloned.1.call-start = ((), (), s32[]{:S(2)}) async-start(), calls=%async_computation.2 | async-start | bytes 5640192 | tf_op jit(solution)/shard_map/all_gather | solution.py:294
  42.2 167.8 %collective-permute-start = (bf16[512,1088]{0,1:T(8,128)(2,1)}, bf16[512,1088]{0,1:T(8,128)(2,1)}, u32[]{:S(2)}, u32[]{:S(2)}) collective-permute-start(bf16[512,1088]{0,1:T(8,128)(2,1)} %bitcast.270), channel_id=1, source_target_pairs={{0,1},{1,0},{2,3},{3,2},{4,5},{5,4},{6,7},{7,6},{8,9},{9,8},{10,11... | collective-permute-start | bytes 3342344 | tf_op jit(solution)/shard_map/ppermute | solution.py:281
  46.2 38.4 %collective-permute-start.5 = (bf16[4,144,1152]{2,1,0:T(8,128)(2,1)}, bf16[4,144,1152]{2,1,0:T(8,128)(2,1)}, u32[]{:S(2)}, u32[]{:S(2)}) collective-permute-start(bf16[4,144,1152]{2,1,0:T(8,128)(2,1)} %pad_maximum_fusion.4.refs_0_), channel_id=1, source_target_pairs={{0,4},{4,0},{8,12},{12,8},{16,20},{20,16},{24,28},{28,24},{1,5},{5... | collective-permute-start | bytes 3981320 | tf_op jit(solution)/shard_map/ppermute | solution.py:275
  49.5 22.0 %collective-permute-start.6 = (bf16[136,1152]{1,0:T(8,128)(2,1)S(1)}, bf16[136,1152]{1,0:T(8,128)(2,1)S(1)}, u32[]{:S(2)}, u32[]{:S(2)}) collective-permute-start(bf16[136,1152]{1,0:T(8,128)(2,1)S(1)} %copy-done.22), channel_id=1, source_target_pairs={{0,8},{4,12},{8,16},{12,20},{16,24},{20,28},{24,0},{28,4},{1,9},{5... | collective-permute-start | bytes 940040 | tf_op jit(solution)/shard_map/ppermute | solution.py:270
  57.1 27.5 %collective-permute-start.7 = (bf16[136,1152]{1,0:T(8,128)(2,1)S(1)}, bf16[136,1152]{1,0:T(8,128)(2,1)S(1)}, u32[]{:S(2)}, u32[]{:S(2)}) collective-permute-start(bf16[136,1152]{1,0:T(8,128)(2,1)S(1)} %copy-done.22), channel_id=1, source_target_pairs={{0,16},{4,20},{8,24},{12,28},{16,0},{20,4},{24,8},{28,12},{1,17},{... | collective-permute-start | bytes 940040 | tf_op jit(solution)/shard_map/ppermute | solution.py:270
  58.7 393.1 %reduce-scatter.2.cloned.1.call-start = ((), (), s32[]{:S(2)}) async-start(), calls=%async_computation.3 | async-start | bytes 5640192 | tf_op jit(solution)/shard_map/reduce_scatter | solution.py:297
  58.8 25.8 %collective-permute-start.8 = (bf16[136,1152]{1,0:T(8,128)(2,1)S(1)}, bf16[136,1152]{1,0:T(8,128)(2,1)S(1)}, u32[]{:S(2)}, u32[]{:S(2)}) collective-permute-start(bf16[136,1152]{1,0:T(8,128)(2,1)S(1)} %copy-done.22), channel_id=1, source_target_pairs={{0,24},{4,28},{8,0},{12,4},{16,8},{20,12},{24,16},{28,20},{1,25},{... | collective-permute-start | bytes 940040 | tf_op jit(solution)/shard_map/ppermute | solution.py:270
  88.9 38.6 %collective-permute-start.10 = (bf16[4,136,1152]{2,1,0:T(8,128)(2,1)S(1)}, bf16[4,136,1152]{2,1,0:T(8,128)(2,1)}, u32[]{:S(2)}, u32[]{:S(2)}) collective-permute-start(bf16[4,136,1152]{2,1,0:T(8,128)(2,1)S(1)} %pad_maximum_fusion.5.refs_0_), channel_id=1, source_target_pairs={{0,4},{4,0},{8,12},{12,8},{16,20},{20,16},{24,28},{28,24},{1,5},{5... | collective-permute-start | bytes 3760136 | tf_op jit(solution)/shard_map/ppermute | solution.py:275
  90.9 36.6 %collective-permute-start.9 = (bf16[2,4,136,576]{3,2,1,0:T(8,128)(2,1)}, bf16[2,4,136,576]{3,2,1,0:T(8,128)(2,1)}, u32[]{:S(2)}, u32[]{:S(2)}) collective-permute-start(bf16[2,4,136,576]{3,2,1,0:T(8,128)(2,1)} %pad_maximum_fusion.3), channel_id=1, source_target_pairs={{0,2},{2,0},{1,3},{3,1},{4,6},{6,4},{5,7},{7,5},{8,10},{10,8},{9,1... | collective-permute-start | bytes 3760136 | tf_op jit(solution)/shard_map/ppermute | solution.py:278
  113.8 56.8 %collective-permute-start.12 = (bf16[1088,576]{0,1:T(8,128)(2,1)}, bf16[1088,576]{0,1:T(8,128)(2,1)}, u32[]{:S(2)}, u32[]{:S(2)}) collective-permute-start(bf16[1088,576]{0,1:T(8,128)(2,1)} %copy.54), channel_id=1, source_target_pairs={{0,1},{1,0},{2,3},{3,2},{4,5},{5,4},{6,7},{7,6},{8,9},{9,8},{10,11... | collective-permute-start | bytes 3760136 | tf_op jit(solution)/shard_map/ppermute | solution.py:281
  130.5 55.6 %collective-permute-start.13 = (bf16[2,4,136,1152]{3,2,1,0:T(8,128)(2,1)}, bf16[2,4,136,1152]{3,2,1,0:T(8,128)(2,1)}, u32[]{:S(2)}, u32[]{:S(2)}) collective-permute-start(bf16[2,4,136,1152]{3,2,1,0:T(8,128)(2,1)} %pad_maximum_fusion.2), channel_id=1, source_target_pairs={{0,2},{2,0},{1,3},{3,1},{4,6},{6,4},{5,7},{7,5},{8,10},{10,8},{9,1... | collective-permute-start | bytes 7520264 | tf_op jit(solution)/shard_map/ppermute | solution.py:278
  240.6 34.5 %collective-permute-start.14 = (f32[1024,1088]{0,1:T(8,128)}, f32[1024,1088]{0,1:T(8,128)}, u32[]{:S(2)}, u32[]{:S(2)}) collective-permute-start(f32[1024,1088]{0,1:T(8,128)} %fusion.86), channel_id=1, source_target_pairs={{0,1},{1,0},{2,3},{3,2},{4,5},{5,4},{6,7},{7,6},{8,9},{9,8},{10,11... | collective-permute-start | bytes 13369352 | tf_op jit(solution)/shard_map/ppermute | solution.py:281
  261.0 30.7 %collective-permute-start.15 = (bf16[2,2,136,1152]{3,2,1,0:T(8,128)(2,1)}, bf16[2,2,136,1152]{3,2,1,0:T(8,128)(2,1)}, u32[]{:S(2)}, u32[]{:S(2)}) collective-permute-start(bf16[2,2,136,1152]{3,2,1,0:T(8,128)(2,1)} %pad_maximum_fusion.6), channel_id=1, source_target_pairs={{0,2},{2,0},{1,3},{3,1},{4,6},{6,4},{5,7},{7,5},{8,10},{10,8},{9,1... | collective-permute-start | bytes 3760136 | tf_op jit(solution)/shard_map/ppermute | solution.py:278
  263.7 59.7 %collective-permute-start.18 = (bf16[2,2,136,1152]{3,2,1,0:T(8,128)(2,1)}, bf16[2,2,136,1152]{3,2,1,0:T(8,128)(2,1)}, u32[]{:S(2)}, u32[]{:S(2)}) collective-permute-start(bf16[2,2,136,1152]{3,2,1,0:T(8,128)(2,1)} %pad_maximum_fusion.7), channel_id=1, source_target_pairs={{0,2},{2,0},{1,3},{3,1},{4,6},{6,4},{5,7},{7,5},{8,10},{10,8},{9,1... | collective-permute-start | bytes 3760136 | tf_op jit(solution)/shard_map/ppermute | solution.py:278
  328.0 45.7 %collective-permute-start.22 = (bf16[4,136,576]{2,1,0:T(8,128)(2,1)}, bf16[4,136,576]{2,1,0:T(8,128)(2,1)}, u32[]{:S(2)}, u32[]{:S(2)}) collective-permute-start(bf16[4,136,576]{2,1,0:T(8,128)(2,1)} %dynamic-slice_bitcast_fusion.2), channel_id=1, source_target_pairs={{0,4},{4,0},{8,12},{12,8},{16,20},{20,16},{24,28},{28,24},{1,5},{5... | collective-permute-start | bytes 1880072 | tf_op jit(solution)/shard_map/ppermute | solution.py:275
  331.4 42.3 %collective-permute-start.19 = (bf16[2,136,1152]{2,1,0:T(8,128)(2,1)}, bf16[2,136,1152]{2,1,0:T(8,128)(2,1)S(1)}, u32[]{:S(2)}, u32[]{:S(2)}) collective-permute-start(bf16[2,136,1152]{2,1,0:T(8,128)(2,1)} %dynamic-slice_bitcast_fusion.3), channel_id=1, source_target_pairs={{0,4},{4,0},{8,12},{12,8},{16,20},{20,16},{24,28},{28,24},{1,5},{5... | collective-permute-start | bytes 1880072 | tf_op jit(solution)/shard_map/ppermute | solution.py:275
  334.8 24.8 %collective-permute-start.20 = (bf16[136,1152]{1,0:T(8,128)(2,1)}, bf16[136,1152]{1,0:T(8,128)(2,1)S(1)}, u32[]{:S(2)}, u32[]{:S(2)}) collective-permute-start(bf16[136,1152]{1,0:T(8,128)(2,1)} %get-tuple-element.197), channel_id=1, source_target_pairs={{0,8},{4,12},{8,16},{12,20},{16,24},{20,28},{24,0},{28,4},{1,9},{5... | collective-permute-start | bytes 940040 | tf_op jit(solution)/shard_map/ppermute | solution.py:270
  335.0 38.6 %collective-permute-start.21 = (bf16[136,1152]{1,0:T(8,128)(2,1)}, bf16[136,1152]{1,0:T(8,128)(2,1)}, u32[]{:S(2)}, u32[]{:S(2)}) collective-permute-start(bf16[136,1152]{1,0:T(8,128)(2,1)} %get-tuple-element.196), channel_id=1, source_target_pairs={{0,16},{4,20},{8,24},{12,28},{16,0},{20,4},{24,8},{28,12},{1,17},{... | collective-permute-start | bytes 940040 | tf_op jit(solution)/shard_map/ppermute | solution.py:270
  384.8 26.1 %collective-permute-start.23 = (bf16[1088,576]{0,1:T(8,128)(2,1)}, bf16[1088,576]{0,1:T(8,128)(2,1)}, u32[]{:S(2)}, u32[]{:S(2)}) collective-permute-start(bf16[1088,576]{0,1:T(8,128)(2,1)} %convolution_convert_fusion.5), channel_id=1, source_target_pairs={{0,2},{2,0},{1,3},{3,1},{4,6},{6,4},{5,7},{7,5},{8,10},{10,8},{9,1... | collective-permute-start | bytes 3760136 | tf_op jit(solution)/shard_map/ppermute | solution.py:278
  450.3 27.9 %collective-permute-start.40 = (bf16[136,1728]{1,0:T(8,128)(2,1)S(1)}, bf16[136,1728]{1,0:T(8,128)(2,1)}, u32[]{:S(2)}, u32[]{:S(2)}) collective-permute-start(bf16[136,1728]{1,0:T(8,128)(2,1)S(1)} %pad_maximum_fusion.8.a_ref), channel_id=1, source_target_pairs={{0,2},{2,0},{1,3},{3,1},{4,6},{6,4},{5,7},{7,5},{8,10},{10,8},{9,1... | collective-permute-start | bytes 1410056 | tf_op jit(solution)/shard_map/ppermute | solution.py:278
  451.8 29.1 %collective-permute-start.43 = (bf16[272,1088]{1,0:T(8,128)(2,1)}, bf16[272,1088]{1,0:T(8,128)(2,1)}, u32[]{:S(2)}, u32[]{:S(2)}) collective-permute-start(bf16[272,1088]{1,0:T(8,128)(2,1)} %reduce-scatter.2.cloned.1.call-done.a_ref), channel_id=1, source_target_pairs={{0,2},{2,0},{1,3},{3,1},{4,6},{6,4},{5,7},{7,5},{8,10},{10,8},{9,1... | collective-permute-start | bytes 1775624 | tf_op jit(solution)/shard_map/ppermute | solution.py:278
  (83 other events, 904.0 us)
Sparse Core Ops, SparseCore 0:
  42.2 68.9 all-gather.2
  113.9 83.0 all-gather.4
  264.3 113.8 reduce-scatter.1

commit v2 on v1

--- a/solution.py
+++ b/solution.py
@@ -556,27 +556,23 @@
         out_cube = rows_cube(grad_wout)
         out_near = grid.near_send(out_cube)
     grad_cube = attend_back(project, info, mixed, grad_mixed, logs, heads)
-    if grid.split:
-        grad_cube, up_near, up_cubes, up_far, out_near, out_cube = hold(
-            (grad_cube, up_near, up_cubes, up_far, out_near, out_cube)
-        )
+    grad_project = grad_cube.reshape(3 * wide, total_len)
+    qkv_sent = product(normed, grad_project[2 * wide :], 0, 1).astype(BF)
+    if grid.split:
+        qkv_keys = product(normed, grad_project[wide : 2 * wide], 0, 1).astype(BF)
+        qkv_mine = product(normed, grad_project[:wide], 0, 1).astype(BF)
+    else:
+        qkv_mine = product(normed, grad_project[: 2 * wide], 0, 1).astype(BF)
+    if grid.split:
+        qkv_sent, qkv_mine, qkv_keys, grad_project, up_near, up_cubes, out_near, out_cube = hold(
+            (qkv_sent, qkv_mine, qkv_keys, grad_project, up_near, up_cubes, out_near, out_cube)
+        )
+        qkv_sent = grid.swap_rep(qkv_sent)
         up_far.update(send_far(1))
         out_far = [
             grid.far_shift(grid.near_sum(out_cube, out_near, k).astype(BF), k)
             for k in range(1, far)
         ]
-    grad_project = grad_cube.reshape(3 * wide, total_len)
-    qkv_sent = product(normed, grad_project[2 * wide :], 0, 1).astype(BF)
-    if grid.split:
-        qkv_keys = product(normed, grad_project[wide : 2 * wide], 0, 1).astype(BF)
-        qkv_mine = product(normed, grad_project[:wide], 0, 1).astype(BF)
-    else:
-        qkv_mine = product(normed, grad_project[: 2 * wide], 0, 1).astype(BF)
-    if grid.split:
-        qkv_sent, qkv_mine, qkv_keys, grad_project = hold(
-            (qkv_sent, qkv_mine, qkv_keys, grad_project)
-        )
-        qkv_sent = grid.swap_rep(qkv_sent)
         key_cube = rows_cube(qkv_keys)
         key_near = grid.near_send(key_cube)
     grad_normed = product(grad_project, full_qkv, 0, 1)
@@ -584,6 +580,8 @@
         qkv_sent, qkv_mine, key_near, key_cube, grad_normed = hold(
             (qkv_sent, qkv_mine, key_near, key_cube, grad_normed)
         )
+        own_down = hold(own_down, qkv_sent)
+        down_other = grid.swap_rep(own_down)
         low = qkv_mine.astype(F32) + qkv_sent.astype(F32)
         low_cube = rows_cube(low.astype(BF))
         low_near = grid.near_send(low_cube)
@@ -592,9 +590,37 @@
     grad_tokens = own_rows(grad_middle) + norm_backward(own_grad, own_scaled, own_inverse, gain_one)
     grad_tokens = grad_tokens.reshape(seqs, rows, width)
 
-    if grid.split:
-        low_near, low_cube, key_near, key_cube, up_far, out_far, own_grad = hold(
-            (low_near, low_cube, key_near, key_cube, up_far, out_far, own_grad)
+    once = jnp.where(first, 1.0, 0.0).astype(F32)
+    spread = lambda values, start, size: lax.dynamic_update_slice(
+        jnp.zeros((size,), F32), values, (start,)
+    )
+    project_sums = jnp.sum(grad_cube.astype(F32), axis=3).reshape(3, wide)
+    sums_q = choose(lead, project_sums[0], project_sums[2])
+    sums_v = choose(lead, project_sums[2], project_sums[0])
+    grad_bias_qv = jnp.concatenate(
+        [spread(sums_q, skip * c, width), spread(sums_v, skip * c, width)]
+    )
+    pre_sums = jnp.sum(grad_pre.astype(F32), axis=0).reshape(count, slab)
+    grad_bias_up = lax.dynamic_update_slice(
+        jnp.zeros((count, 2, slab), F32), pre_sums[:, None], (0, c, 0)
+    )
+    vectors = [
+        jnp.sum(own_grad * own_scaled, axis=0),
+        jnp.sum(own_grad, axis=0),
+        grad_bias_qv,
+        once * jnp.sum(grad_branch.astype(F32), axis=0),
+        once * jnp.sum(grad_hidden * scaled_two, axis=0),
+        once * jnp.sum(grad_hidden, axis=0),
+        grad_bias_up,
+        once * jnp.sum(all_cot.astype(F32), axis=0),
+    ]
+    table = jnp.concatenate([v.reshape(count, -1) for v in vectors], axis=1)
+    table = table + grid.swap_ctx(table)
+    table = table + grid.swap_rep(table) if grid.split else lax.psum(table, "rep")
+
+    if grid.split:
+        low_near, low_cube, key_near, key_cube, own_grad = hold(
+            (low_near, low_cube, key_near, key_cube, own_grad)
         )
         key_far = [
             grid.far_shift(grid.near_sum(key_cube, key_near, k).astype(BF), k)
@@ -621,7 +647,6 @@
             up_wide,
             skip,
         )
-        down_other = grid.swap_rep(own_down)
         out_down = finish_down(
             places,
             (own_down, down_other),
@@ -684,33 +709,6 @@
         pieces.append(high_qkv[:, k * wide : (k + 1) * wide])
     out_qkv = jnp.concatenate(pieces, axis=1).astype(F32)
 
-    once = jnp.where(first, 1.0, 0.0).astype(F32)
-    spread = lambda values, start, size: lax.dynamic_update_slice(
-        jnp.zeros((size,), F32), values, (start,)
-    )
-    project_sums = jnp.sum(grad_cube.astype(F32), axis=3).reshape(3, wide)
-    sums_q = choose(lead, project_sums[0], project_sums[2])
-    sums_v = choose(lead, project_sums[2], project_sums[0])
-    grad_bias_qv = jnp.concatenate(
-        [spread(sums_q, skip * c, width), spread(sums_v, skip * c, width)]
-    )
-    pre_sums = jnp.sum(grad_pre.astype(F32), axis=0).reshape(count, slab)
-    grad_bias_up = lax.dynamic_update_slice(
-        jnp.zeros((count, 2, slab), F32), pre_sums[:, None], (0, c, 0)
-    )
-    vectors = [
-        jnp.sum(own_grad * own_scaled, axis=0),
-        jnp.sum(own_grad, axis=0),
-        grad_bias_qv,
-        once * jnp.sum(grad_branch.astype(F32), axis=0),
-        once * jnp.sum(grad_hidden * scaled_two, axis=0),
-        once * jnp.sum(grad_hidden, axis=0),
-        grad_bias_up,
-        once * jnp.sum(all_cot.astype(F32), axis=0),
-    ]
-    table = jnp.concatenate([v.reshape(count, -1) for v in vectors], axis=1)
-    table = table + grid.swap_ctx(table)
-    table = table + grid.swap_rep(table) if grid.split else lax.psum(table, "rep")
     summed = grid.scatter(table[:, None, :]).reshape(-1)
     outs, at = [], 0
     for size in sizes:

time: 536 us -> 529 us (0.987)
  waiting for transfers between devices: 129 us -> 114 us
  starting transfers between devices: 57.3 us -> 70.6 us
    ppermute x21, starting transfers between devices: 36.5 us -> 50.9 us  [far_shift(): return lax.ppermute(array, 'fsdp', pairs)]
    ppermute x21, waiting for transfers between devices: 47.4 us -> 35.6 us  [far_shift(): return lax.ppermute(array, 'fsdp', pairs)]
  transfers between devices with their start and end apart: 55 -> 55, of which waited for: 20 -> 16; matrix products, arithmetic and copies ran while one was open for 43% -> 42% of each run, Pallas kernels for 12% -> 12%
where the time goes in v2:
time: 529 us; the launch traced here: 520 us
  waiting for transfers between devices  114 us (22%)
  matrix products  95.5 us (18%)
  local copies, waits for them, and re-layouts  81.4 us (15%)
  other arithmetic  79.4 us (15%)
  starting transfers between devices  70.6 us (13%)
  Pallas kernels  63.1 us (12%)
  between operations  16.1 us (3%)
    dot_general x15, matrix products, product(): lax.dot_general(left, right, (((left_dim,), (right_dim,)), ((), ())), pre...  95.5 us
    ppermute x21, starting transfers between devices, far_shift(): return lax.ppermute(array, 'fsdp', pairs)  50.9 us
    ppermute x10, waiting for transfers between devices, swap_rep(): return lax.ppermute(array, 'rep', [(0, 1), (1, 0)])  37.8 us
    ppermute x21, waiting for transfers between devices, far_shift(): return lax.ppermute(array, 'fsdp', pairs)  35.6 us
    ppermute x8, waiting for transfers between devices, near_shift(): return lax.ppermute(array, 'fsdp', pairs)  28.7 us
    pallas_call x1, Pallas kernels, attend_back(): pl.pallas_call(bwd_kernel, out_shape=jax.ShapeDtypeStruct((3, heads, HD,...  22.4 us
    pallas_call x1, Pallas kernels, attend(): pl.pallas_call(fwd_kernel, out_shape=(jax.ShapeDtypeStruct((heads, HD, to...  22 us
    all_gather x2, waiting for transfers between devices, gather_all(): return lax.all_gather(piece, 'fsdp', axis=0, tiled=True)  11.4 us
  transfers between devices with their start and end apart: 55, of which 16 were waited for; matrix products, arithmetic and copies ran while one was open for 42% of the time, Pallas kernels for 12%

profile of v2, /device:TPU:0, one launch (start us, length us, event | category | flops | bytes accessed | tf_op | source)
XLA Modules:
  0.0 519.7 jit_solution(6959777390687818152)
XLA Ops:
  21.7 6.4 %reshape.404 = bf16[136,8,2,272]{3,2,1,0:T(2,128)(2,1)} reshape(bf16[136,4352]{1,0:T(8,128)(2,1)} %param.25) | data formatting | bytes 2367488 | tf_op jit(solution)/shard_map/reshape | solution.py:397
  28.0 6.7 %dynamic-slice_reduce_fusion = bf16[136,8,272]{2,1,0:T(8,128)(2,1)S(1)} fusion(bf16[136,8,2,272]{3,2,1,0:T(2,128)(2,1)} %reshape.404, s32[]{:T(128)S(6)} %select_n.385), kind=kLoop, calls=%fused_computation.67 | loop fusion | bytes 1183748 | tf_op jit(solution)/shard_map/jit(dynamic_index_in_dim)/dynamic_slice | solution.py:398
  49.9 7.6 %collective-permute-start.6 = (bf16[136,1152]{1,0:T(8,128)(2,1)S(1)}, bf16[136,1152]{1,0:T(8,128)(2,1)S(1)}, u32[]{:S(2)}, u32[]{:S(2)}) collective-permute-start(bf16[136,1152]{1,0:T(8,128)(2,1)S(1)} %copy-done.21), channel_id=1, source_target_pairs={{0,8},{4,12},{8,16},{12,20},{16,24},{20,28},{24,0},{28,4},{1,9},{5... | collective-permute-start | bytes 940040 | tf_op jit(solution)/shard_map/ppermute | solution.py:270
  61.9 10.4 %collective-permute-done.6 = bf16[136,1152]{1,0:T(8,128)(2,1)S(1)} collective-permute-done((bf16[136,1152]{1,0:T(8,128)(2,1)S(1)}, bf16[136,1152]{1,0:T(8,128)(2,1)S(1)}, u32[]{:S(2)}, u32[]{:S(2)}) %collective-permute-start.6) | collective-permute-done | bytes 313376 | tf_op jit(solution)/shard_map/ppermute | solution.py:270
  72.3 12.7 %collective-permute-done.7 = bf16[136,1152]{1,0:T(8,128)(2,1)S(1)} collective-permute-done((bf16[136,1152]{1,0:T(8,128)(2,1)S(1)}, bf16[136,1152]{1,0:T(8,128)(2,1)S(1)}, u32[]{:S(2)}, u32[]{:S(2)}) %collective-permute-start.7) | collective-permute-done | bytes 313376 | tf_op jit(solution)/shard_map/ppermute | solution.py:270
  100.2 11.4 %all-gather.3.cloned.1.call-done = bf16[1088,576]{1,0:T(8,128)(2,1)} async-done(((bf16[136,576]{1,0:T(8,128)(2,1)}), bf16[1088,576]{1,0:T(8,128)(2,1)}) %all-gather.3.cloned.1.call-update) | async-done | bytes 1253392 | tf_op jit(solution)/shard_map/all_gather | solution.py:294
  114.2 13.8 %collective-permute-done.10.refs_1_ = bf16[4,136,1152]{2,1,0:T(8,128)(2,1)} collective-permute-done((bf16[4,136,1152]{2,1,0:T(8,128)(2,1)S(1)}, bf16[4,136,1152]{2,1,0:T(8,128)(2,1)}, u32[]{:S(2)}, u32[]{:S(2)}) %collective-permute-start.10) | collective-permute-done | bytes 1253408 | tf_op jit(solution)/shard_map/ppermute | solution.py:275
  137.4 9.4 %add_convert_fusion = bf16[1728,1024]{1,0:T(8,128)(2,1)} fusion(bf16[1088,1728]{1,0:T(8,128)(2,1)} %bitcast.261, bf16[1024,1088]{0,1:T(8,128)(2,1)} %fusion.11, f32[1728]{0:T(1024)S(1)} %concatenate.65), kind=kOutput, calls=%fused_computation.14 | convolution fusion | flops 3853910016 | bytes 9534208 | tf_op jit(solution)/shard_map/dot_general | solution.py:112
  146.8 22.0 %attend.1 = (bf16[9,64,1024]{2,1,0:T(8,128)(2,1)}, f32[9,1,1024]{2,1,0:T(1,128)}) custom-call(s32[4]{0:T(128)} %pad_add_fusion.info, bf16[27,64,1024]{2,1,0:T(8,128)(2,1)} %bitcast.288, bf16[27,64,1024]{2,1,0:T(8,128)(2,1)} %bitcast.289, bf16[27,64,1024]{2,1,0:T(8,128)(2,1)} %bitcast.290), custom_call_target="tpu_custom_call" | custom-call | flops 2415919104 | bytes 4718592 | tf_op jit(solution)/shard_map/attend/pallas_call | solution.py:82
  179.1 7.0 %fusion.7 = f32[1024,1088]{0,1:T(8,128)} fusion(bf16[1088,512]{1,0:T(8,128)(2,1)S(1)} %slice_select_fusion, bf16[1088,576]{1,0:T(8,128)(2,1)S(1)} %broadcast_select_fusion, f32[1088]{0:T(1024)S(1)} %copy-done.54, bf16[512,1024]{1,0:T(8,128)(2,1)S(1)} %slice.221, bf16[576,1024]{1,0:T(8,128)(2,1)S(1)} %bitcast.277, bf16[512,1024]{1,0:T(8,128)(2,1)S(1)} %bitcast.274, ...), kind=kOutput, calls=%fused_computation.22 | convolution fusion | flops 2452439040 | bytes 13512961 | tf_op jit(solution)/shard_map/dot_general | solution.py:112
  201.1 9.3 %multiply_convert_fusion.1 = (bf16[1024,2176]{1,0:T(8,128)(2,1)S(1)}, f32[1024,2176]{1,0:T(8,128)}) fusion(f32[2176]{0:T(1024)S(1)} %add.583, bf16[1024,1088]{0,1:T(8,128)(2,1)S(1)} %add_convert_fusion.1, bf16[1088,2176]{1,0:T(8,128)(2,1)S(1)} %bitcast.257), kind=kOutput, calls=%fused_computation.9 | convolution fusion | flops 4861984768 | bytes 20341248 | tf_op jit(solution)/shard_map/dot_general | solution.py:112
  212.4 9.6 %convolution_convert_fusion = bf16[2176,1088]{1,0:T(8,128)(2,1)} fusion(bf16[1024,2176]{1,0:T(8,128)(2,1)S(1)} %get-tuple-element.205, bf16[512,1088]{0,1:T(8,128)(2,1)} %collective-permute-done, bf16[512,1088]{0,1:T(8,128)(2,1)S(1)} %bitcast.271, pred[]{:T(512)S(6)} %eq.72), kind=kOutput, calls=%fused_computation.1 | convolution fusion | flops 4861009920 | bytes 11419649 | tf_op jit(solution)/shard_map/dot_general | solution.py:112
  222.1 11.5 %convert_reduce_fusion = (f32[2176]{0:T(1024)S(1)}, bf16[1024,2176]{1,0:T(8,128)(2,1)S(1)}) fusion(f32[1024,2176]{1,0:T(8,128)} %get-tuple-element.206, f32[2176]{0:T(1024)S(1)} %add.583, bf16[2176,1088]{1,0:T(8,128)(2,1)} %all-gather.5.cloned.1.call-done, bf16[512,1088]{0,1:T(8,128)(2,1)} %collective-permute-done, bf16[512,1088]{0,1:T(8,128)(2,1)S(1)} %bitcast.272, ...), kind=kOutput, calls=%fused_computation.7 | convolution fusion | flops 4892063744 | bytes 20349952 | tf_op jit(solution)/shard_map/dot_general | solution.py:112
  233.7 7.4 %fusion.85 = f32[1024,1088]{0,1:T(8,128)} fusion(bf16[1024,2176]{1,0:T(8,128)(2,1)S(1)} %get-tuple-element.208, bf16[1088,2176]{1,0:T(8,128)(2,1)S(1)} %bitcast.260), kind=kOutput, calls=%fused_computation.223 | convolution fusion | flops 4848615424 | bytes 13647872 | tf_op jit(solution)/shard_map/dot_general | solution.py:112
  276.8 11.9 %collective-permute-done.15 = bf16[2,2,136,1152]{3,2,1,0:T(8,128)(2,1)} collective-permute-done((bf16[2,2,136,1152]{3,2,1,0:T(8,128)(2,1)}, bf16[2,2,136,1152]{3,2,1,0:T(8,128)(2,1)}, u32[]{:S(2)}, u32[]{:S(2)}) %collective-permute-start.15) | collective-permute-done | bytes 1253408 | tf_op jit(solution)/shard_map/ppermute | solution.py:278
  295.6 6.5 %fusion.80 = (bf16[1024,1088]{0,1:T(8,128)(2,1)}, f32[1024,1088]{0,1:T(8,128)}, f32[1088]{0:T(1024)S(1)}) fusion(f32[1024]{0:T(1024)S(1)} %broadcast_multiply_fusion.4, f32[1024,1088]{0,1:T(8,128)S(1)} %bitcast.239, f32[1024]{0:T(1024)S(1)} %broadcast_multiply_fusion.6, f32[1024]{0:T(1024)S(1)} %broadcast_multiply_fusion.5, f32[1024,1088]{0,1:T(8,128)S(1)} %add.588, ...), kind=kLoop, calls=%fused_computation.218 | loop fusion | flops 22281152 | bytes 17850880 | tf_op jit(solution)/shard_map/convert_element_type | solution.py:537
  304.2 7.8 %collective-permute-done.17 = bf16[2,136,1152]{2,1,0:T(8,128)(2,1)} collective-permute-done((bf16[2,136,1152]{2,1,0:T(8,128)(2,1)}, bf16[2,136,1152]{2,1,0:T(8,128)(2,1)}, u32[]{:S(2)}, u32[]{:S(2)}) %collective-permute-start.17) | collective-permute-done | bytes 626720 | tf_op jit(solution)/shard_map/ppermute | solution.py:275
  330.2 22.4 %attend_back.1 = bf16[3,9,64,1024]{3,2,1,0:T(8,128)(2,1)} custom-call(s32[4]{0:T(128)} %pad_add_fusion.info, bf16[27,64,1024]{2,1,0:T(8,128)(2,1)} %bitcast.291, bf16[27,64,1024]{2,1,0:T(8,128)(2,1)} %bitcast.292, bf16[27,64,1024]{2,1,0:T(8,128)(2,1)} %bitcast.293, bf16[9,64,1024]{2,1,0:T(8,128)(2,1)} %get-tuple-element.92.o_ref, ...), custom_call_target="tpu_custom_call" | custom-call | flops 6039797760 | bytes 9437184 | tf_op jit(solution)/shard_map/attend_back/pallas_call | solution.py:96
  377.2 7.4 %fusion.87 = f32[1024,1088]{0,1:T(8,128)S(1)} fusion(bf16[1088,1728]{1,0:T(8,128)(2,1)} %bitcast.262, bf16[1728,1024]{1,0:T(8,128)(2,1)} %bitcast.245), kind=kOutput, calls=%fused_computation.225 | convolution fusion | flops 3850371072 | bytes 11755520 | tf_op jit(solution)/shard_map/dot_general | solution.py:112
  391.5 8.4 %collective-permute-start.35 = (bf16[136,1152]{1,0:T(8,128)(2,1)S(1)}, bf16[136,1152]{1,0:T(8,128)(2,1)S(1)}, u32[]{:S(2)}, u32[]{:S(2)}) collective-permute-start(bf16[136,1152]{1,0:T(8,128)(2,1)S(1)} %get-tuple-element.179), channel_id=1, source_target_pairs={{0,8},{4,12},{8,16},{12,20},{16,24},{20,28},{24,0},{28,4},{1,9},{5... | collective-permute-start | bytes 940040 | tf_op jit(solution)/shard_map/ppermute | solution.py:270
  410.3 6.1 %collective-permute-done.36 = bf16[136,1152]{1,0:T(8,128)(2,1)S(1)} collective-permute-done((bf16[136,1152]{1,0:T(8,128)(2,1)S(1)}, bf16[136,1152]{1,0:T(8,128)(2,1)S(1)}, u32[]{:S(2)}, u32[]{:S(2)}) %collective-permute-start.36) | collective-permute-done | bytes 313376 | tf_op jit(solution)/shard_map/ppermute | solution.py:270
  421.9 8.9 %collective-permute-done.40.b_ref = bf16[136,1728]{1,0:T(8,128)(2,1)S(1)} collective-permute-done((bf16[136,1728]{1,0:T(8,128)(2,1)S(1)}, bf16[136,1728]{1,0:T(8,128)(2,1)S(1)}, u32[]{:S(2)}, u32[]{:S(2)}) %collective-permute-start.40) | collective-permute-done | bytes 470048 | tf_op jit(solution)/shard_map/ppermute | solution.py:278
  449.6 7.1 %collective-permute-done.30 = bf16[4,136,576]{2,1,0:T(8,128)(2,1)S(1)} collective-permute-done((bf16[4,136,576]{2,1,0:T(8,128)(2,1)}, bf16[4,136,576]{2,1,0:T(8,128)(2,1)S(1)}, u32[]{:S(2)}, u32[]{:S(2)}) %collective-permute-start.30) | collective-permute-done | bytes 626720 | tf_op jit(solution)/shard_map/ppermute | solution.py:275
  471.5 9.4 %collective-permute-done.25 = f32[8,1632]{1,0:T(8,128)S(1)} collective-permute-done((f32[8,1632]{1,0:T(8,128)S(1)}, f32[8,1632]{1,0:T(8,128)S(1)}, u32[]{:S(2)}, u32[]{:S(2)}) %collective-permute-start.25) | collective-permute-done | bytes 52256 | tf_op jit(solution)/shard_map/ppermute | solution.py:278
  (395 shorter events, 262.5 us)
Async XLA Ops:
  7.2 104.4 %all-gather.3.cloned.1.call-start = ((), (), s32[]{:S(2)}) async-start(), calls=%async_computation.1 | async-start | bytes 1566720 | tf_op jit(solution)/shard_map/all_gather | solution.py:294
  14.6 25.9 %collective-permute-start.2 = (bf16[144,1152]{1,0:T(8,128)(2,1)S(1)}, bf16[144,1152]{1,0:T(8,128)(2,1)}, u32[]{:S(2)}, u32[]{:S(2)}) collective-permute-start(bf16[144,1152]{1,0:T(8,128)(2,1)S(1)} %concatenate.63), channel_id=1, source_target_pairs={{0,8},{4,12},{8,16},{12,20},{16,24},{20,28},{24,0},{28,4},{1,9},{5... | collective-permute-start | bytes 995336 | tf_op jit(solution)/shard_map/ppermute | solution.py:270
  17.7 24.3 %collective-permute-start.3 = (bf16[144,1152]{1,0:T(8,128)(2,1)S(1)}, bf16[144,1152]{1,0:T(8,128)(2,1)}, u32[]{:S(2)}, u32[]{:S(2)}) collective-permute-start(bf16[144,1152]{1,0:T(8,128)(2,1)S(1)} %concatenate.63), channel_id=1, source_target_pairs={{0,16},{4,20},{8,24},{12,28},{16,0},{20,4},{24,8},{28,12},{1,17},{... | collective-permute-start | bytes 995336 | tf_op jit(solution)/shard_map/ppermute | solution.py:270
  42.0 180.0 %all-gather.5.cloned.1.call-start = ((), (), s32[]{:S(2)}) async-start(), calls=%async_computation.2 | async-start | bytes 5640192 | tf_op jit(solution)/shard_map/all_gather | solution.py:294
  42.2 168.2 %collective-permute-start = (bf16[512,1088]{0,1:T(8,128)(2,1)}, bf16[512,1088]{0,1:T(8,128)(2,1)}, u32[]{:S(2)}, u32[]{:S(2)}) collective-permute-start(bf16[512,1088]{0,1:T(8,128)(2,1)} %bitcast.270), channel_id=1, source_target_pairs={{0,1},{1,0},{2,3},{3,2},{4,5},{5,4},{6,7},{7,6},{8,9},{9,8},{10,11... | collective-permute-start | bytes 3342344 | tf_op jit(solution)/shard_map/ppermute | solution.py:281
  47.1 38.0 %collective-permute-start.5 = (bf16[4,144,1152]{2,1,0:T(8,128)(2,1)}, bf16[4,144,1152]{2,1,0:T(8,128)(2,1)}, u32[]{:S(2)}, u32[]{:S(2)}) collective-permute-start(bf16[4,144,1152]{2,1,0:T(8,128)(2,1)} %pad_maximum_fusion.4.refs_0_), channel_id=1, source_target_pairs={{0,4},{4,0},{8,12},{12,8},{16,20},{20,16},{24,28},{28,24},{1,5},{5... | collective-permute-start | bytes 3981320 | tf_op jit(solution)/shard_map/ppermute | solution.py:275
  57.5 27.5 %collective-permute-start.7 = (bf16[136,1152]{1,0:T(8,128)(2,1)S(1)}, bf16[136,1152]{1,0:T(8,128)(2,1)S(1)}, u32[]{:S(2)}, u32[]{:S(2)}) collective-permute-start(bf16[136,1152]{1,0:T(8,128)(2,1)S(1)} %copy-done.21), channel_id=1, source_target_pairs={{0,16},{4,20},{8,24},{12,28},{16,0},{20,4},{24,8},{28,12},{1,17},{... | collective-permute-start | bytes 940040 | tf_op jit(solution)/shard_map/ppermute | solution.py:270
  59.1 403.8 %reduce-scatter.2.cloned.1.call-start = ((), (), s32[]{:S(2)}) async-start(), calls=%async_computation.3 | async-start | bytes 5640192 | tf_op jit(solution)/shard_map/reduce_scatter | solution.py:297
  59.2 25.8 %collective-permute-start.8 = (bf16[136,1152]{1,0:T(8,128)(2,1)S(1)}, bf16[136,1152]{1,0:T(8,128)(2,1)S(1)}, u32[]{:S(2)}, u32[]{:S(2)}) collective-permute-start(bf16[136,1152]{1,0:T(8,128)(2,1)S(1)} %copy-done.21), channel_id=1, source_target_pairs={{0,24},{4,28},{8,0},{12,4},{16,8},{20,12},{24,16},{28,20},{1,25},{... | collective-permute-start | bytes 940040 | tf_op jit(solution)/shard_map/ppermute | solution.py:270
  89.4 38.6 %collective-permute-start.10 = (bf16[4,136,1152]{2,1,0:T(8,128)(2,1)S(1)}, bf16[4,136,1152]{2,1,0:T(8,128)(2,1)}, u32[]{:S(2)}, u32[]{:S(2)}) collective-permute-start(bf16[4,136,1152]{2,1,0:T(8,128)(2,1)S(1)} %pad_maximum_fusion.5.refs_0_), channel_id=1, source_target_pairs={{0,4},{4,0},{8,12},{12,8},{16,20},{20,16},{24,28},{28,24},{1,5},{5... | collective-permute-start | bytes 3760136 | tf_op jit(solution)/shard_map/ppermute | solution.py:275
  91.3 36.7 %collective-permute-start.9 = (bf16[2,4,136,576]{3,2,1,0:T(8,128)(2,1)}, bf16[2,4,136,576]{3,2,1,0:T(8,128)(2,1)}, u32[]{:S(2)}, u32[]{:S(2)}) collective-permute-start(bf16[2,4,136,576]{3,2,1,0:T(8,128)(2,1)} %pad_maximum_fusion.3), channel_id=1, source_target_pairs={{0,2},{2,0},{1,3},{3,1},{4,6},{6,4},{5,7},{7,5},{8,10},{10,8},{9,1... | collective-permute-start | bytes 3760136 | tf_op jit(solution)/shard_map/ppermute | solution.py:278
  114.2 56.9 %collective-permute-start.12 = (bf16[1088,576]{0,1:T(8,128)(2,1)}, bf16[1088,576]{0,1:T(8,128)(2,1)}, u32[]{:S(2)}, u32[]{:S(2)}) collective-permute-start(bf16[1088,576]{0,1:T(8,128)(2,1)} %copy.54), channel_id=1, source_target_pairs={{0,1},{1,0},{2,3},{3,2},{4,5},{5,4},{6,7},{7,6},{8,9},{9,8},{10,11... | collective-permute-start | bytes 3760136 | tf_op jit(solution)/shard_map/ppermute | solution.py:281
  131.0 55.5 %collective-permute-start.13 = (bf16[2,4,136,1152]{3,2,1,0:T(8,128)(2,1)}, bf16[2,4,136,1152]{3,2,1,0:T(8,128)(2,1)}, u32[]{:S(2)}, u32[]{:S(2)}) collective-permute-start(bf16[2,4,136,1152]{3,2,1,0:T(8,128)(2,1)} %pad_maximum_fusion.2), channel_id=1, source_target_pairs={{0,2},{2,0},{1,3},{3,1},{4,6},{6,4},{5,7},{7,5},{8,10},{10,8},{9,1... | collective-permute-start | bytes 7520264 | tf_op jit(solution)/shard_map/ppermute | solution.py:278
  241.1 31.0 %collective-permute-start.14 = (f32[1024,1088]{0,1:T(8,128)}, f32[1024,1088]{0,1:T(8,128)}, u32[]{:S(2)}, u32[]{:S(2)}) collective-permute-start(f32[1024,1088]{0,1:T(8,128)} %fusion.85), channel_id=1, source_target_pairs={{0,1},{1,0},{2,3},{3,2},{4,5},{5,4},{6,7},{7,6},{8,9},{9,8},{10,11... | collective-permute-start | bytes 13369352 | tf_op jit(solution)/shard_map/ppermute | solution.py:281
  258.0 30.7 %collective-permute-start.15 = (bf16[2,2,136,1152]{3,2,1,0:T(8,128)(2,1)}, bf16[2,2,136,1152]{3,2,1,0:T(8,128)(2,1)}, u32[]{:S(2)}, u32[]{:S(2)}) collective-permute-start(bf16[2,2,136,1152]{3,2,1,0:T(8,128)(2,1)} %pad_maximum_fusion.6), channel_id=1, source_target_pairs={{0,2},{2,0},{1,3},{3,1},{4,6},{6,4},{5,7},{7,5},{8,10},{10,8},{9,1... | collective-permute-start | bytes 3760136 | tf_op jit(solution)/shard_map/ppermute | solution.py:278
  260.7 60.2 %collective-permute-start.18 = (bf16[2,2,136,1152]{3,2,1,0:T(8,128)(2,1)}, bf16[2,2,136,1152]{3,2,1,0:T(8,128)(2,1)}, u32[]{:S(2)}, u32[]{:S(2)}) collective-permute-start(bf16[2,2,136,1152]{3,2,1,0:T(8,128)(2,1)} %pad_maximum_fusion.7), channel_id=1, source_target_pairs={{0,2},{2,0},{1,3},{3,1},{4,6},{6,4},{5,7},{7,5},{8,10},{10,8},{9,1... | collective-permute-start | bytes 3760136 | tf_op jit(solution)/shard_map/ppermute | solution.py:278
  323.6 42.1 %collective-permute-start.19 = (bf16[2,136,1152]{2,1,0:T(8,128)(2,1)}, bf16[2,136,1152]{2,1,0:T(8,128)(2,1)}, u32[]{:S(2)}, u32[]{:S(2)}) collective-permute-start(bf16[2,136,1152]{2,1,0:T(8,128)(2,1)} %dynamic-slice_bitcast_fusion.3), channel_id=1, source_target_pairs={{0,4},{4,0},{8,12},{12,8},{16,20},{20,16},{24,28},{28,24},{1,5},{5... | collective-permute-start | bytes 1880072 | tf_op jit(solution)/shard_map/ppermute | solution.py:275
  328.8 36.9 %collective-permute-start.20 = (bf16[4,136,576]{2,1,0:T(8,128)(2,1)}, bf16[4,136,576]{2,1,0:T(8,128)(2,1)S(1)}, u32[]{:S(2)}, u32[]{:S(2)}) collective-permute-start(bf16[4,136,576]{2,1,0:T(8,128)(2,1)} %dynamic-slice_bitcast_fusion.2), channel_id=1, source_target_pairs={{0,4},{4,0},{8,12},{12,8},{16,20},{20,16},{24,28},{28,24},{1,5},{5... | collective-permute-start | bytes 1880072 | tf_op jit(solution)/shard_map/ppermute | solution.py:275
  369.7 34.4 %collective-permute-start.22 = (bf16[4,136,576]{2,1,0:T(8,128)(2,1)S(1)}, bf16[4,136,576]{2,1,0:T(8,128)(2,1)S(1)}, u32[]{:S(2)}, u32[]{:S(2)}) collective-permute-start(bf16[4,136,576]{2,1,0:T(8,128)(2,1)S(1)} %dynamic-slice_bitcast_fusion.1), channel_id=1, source_target_pairs={{0,4},{4,0},{8,12},{12,8},{16,20},{20,16},{24,28},{28,24},{1,5},{5... | collective-permute-start | bytes 1880072 | tf_op jit(solution)/shard_map/ppermute | solution.py:275
  370.4 33.6 %collective-permute-start.21 = (bf16[1088,576]{0,1:T(8,128)(2,1)}, bf16[1088,576]{0,1:T(8,128)(2,1)S(1)}, u32[]{:S(2)}, u32[]{:S(2)}) collective-permute-start(bf16[1088,576]{0,1:T(8,128)(2,1)} %convolution_convert_fusion.5), channel_id=1, source_target_pairs={{0,2},{2,0},{1,3},{3,1},{4,6},{6,4},{5,7},{7,5},{8,10},{10,8},{9,1... | collective-permute-start | bytes 3760136 | tf_op jit(solution)/shard_map/ppermute | solution.py:278
  375.6 24.3 %collective-permute-start.39 = (bf16[136,576]{1,0:T(8,128)(2,1)S(1)}, bf16[136,576]{1,0:T(8,128)(2,1)S(1)}, u32[]{:S(2)}, u32[]{:S(2)}) collective-permute-start(bf16[136,576]{1,0:T(8,128)(2,1)S(1)} %get-tuple-element.173), channel_id=1, source_target_pairs={{0,24},{4,28},{8,0},{12,4},{16,8},{20,12},{24,16},{28,20},{1,25},{... | collective-permute-start | bytes 470024 | tf_op jit(solution)/shard_map/ppermute | solution.py:270
  386.0 24.3 %collective-permute-start.34 = (bf16[136,1152]{1,0:T(8,128)(2,1)S(1)}, bf16[136,1152]{1,0:T(8,128)(2,1)S(1)}, u32[]{:S(2)}, u32[]{:S(2)}) collective-permute-start(bf16[136,1152]{1,0:T(8,128)(2,1)S(1)} %copy-done.37), channel_id=1, source_target_pairs={{0,16},{4,20},{8,24},{12,28},{16,0},{20,4},{24,8},{28,12},{1,17},{... | collective-permute-start | bytes 940040 | tf_op jit(solution)/shard_map/ppermute | solution.py:270
  405.9 39.3 %collective-permute-start.23 = (f32[512,1088]{0,1:T(8,128)}, f32[512,1088]{0,1:T(8,128)}, u32[]{:S(2)}, u32[]{:S(2)}) collective-permute-start(f32[512,1088]{0,1:T(8,128)} %constant_dynamic-slice_fusion.8), channel_id=1, source_target_pairs={{0,1},{1,0},{2,3},{3,2},{4,5},{5,4},{6,7},{7,6},{8,9},{9,8},{10,11... | collective-permute-start | bytes 6684680 | tf_op jit(solution)/shard_map/ppermute | solution.py:281
  458.8 24.7 %collective-permute-start.48 = (bf16[136,576]{1,0:T(8,128)(2,1)S(1)}, bf16[136,576]{1,0:T(8,128)(2,1)S(1)}, u32[]{:S(2)}, u32[]{:S(2)}) collective-permute-start(bf16[136,576]{1,0:T(8,128)(2,1)S(1)} %get-tuple-element.170), channel_id=1, source_target_pairs={{0,24},{4,28},{8,0},{12,4},{16,8},{20,12},{24,16},{28,20},{1,25},{... | collective-permute-start | bytes 470024 | tf_op jit(solution)/shard_map/ppermute | solution.py:270
  (94 other events, 992.4 us)
Sparse Core Ops, SparseCore 0:
  42.2 69.3 all-gather.2
  114.3 83.1 all-gather.4
  261.3 110.3 reduce-scatter.1
